TPU v7x, 128 devices: a whole 4x4x4 slice. The times are simulated.
128 devices in a mesh: grp: 8 (over y_lo, x), inner: 16 (over y_hi, z, core).
Axes of the slice: x: 4, y: 4 (y_hi: 2, y_lo: 2; y = y_hi * 2 + y_lo), z: 4, core: 2. Of those that a mesh axis runs over, the one named last changes fastest.
Arguments:
- embeds: bfloat16 [16384, 1024], P(('grp', 'inner')), may hold values from -1.05 to 1.05
- fine_centroids: bfloat16 [16384, 1024], P('inner'), may hold values from -1.05 to 1.05
- coarse_centroids: bfloat16 [512, 1024], replicated, may hold values from -0.39375 to 0.39375
Outputs:
- fine_update: float32 [16384, 1024], P('inner')
- coarse_update: float32 [512, 1024], replicated
All inputs are finite; a program needn't handle non-finite values.
Results may differ from a plain program's by a relative error of at most 0.0044.
Values may be sent and summed in bfloat16 or wider, within the bound.
No kernel may reach another device: no remote copies, remote signals or barrier semaphores. Data moves between devices by JAX's collectives and lax.ppermute only.
A program may use at most 64 MiB of HBM per device.

v0:
```python
import numpy as np
import jax
import jax.numpy as jnp
from jax import lax
from jax.experimental import pallas as pl
from jax.experimental.pallas import tpu as pltpu
from jax.sharding import Mesh
from jax.sharding import PartitionSpec as P

GRP = ("yl", "x")
INNER = ("yh", "z", "c")
CHIPS = ("yl", "x", "yh", "z")
SIZES = {"yl": 2, "x": 4, "yh": 2, "z": 4, "c": 2}

F32 = jnp.float32
BF16 = jnp.bfloat16
shrink = 1.0
anchor = 8.0
inv_temper = 50.0
ROWS_OUT = 136
NT = (((1,), (1,)), ((), ()))
TN = (((0,), (0,)), ((), ()))
VMEM = pltpu.VMEM

CHUNKS = (
    ((0, 0, 0), (0, 0, 1)),
    ((1, 0, 0), (1, 0, 1)),
    ((0, 1, 0), (0, 1, 1), (0, 3, 0), (0, 3, 1)),
    ((1, 1, 0), (1, 1, 1), (1, 3, 0), (1, 3, 1)),
    ((0, 2, 0), (0, 2, 1), (1, 2, 0), (1, 2, 1)),
)
PIECES = tuple(p for chunk in CHUNKS for p in chunk)
NP = len(PIECES)
S_K, S_P, S_C, S_J = 0, 8, 24, 25


def moved(x, axes, shifts):
    sizes = [SIZES[a] for a in axes]
    perm = []
    for idx in np.ndindex(*sizes):
        to = [(i + s) % n for i, s, n in zip(idx, shifts, sizes)]
        perm.append((int(np.ravel_multi_index(idx, sizes)), int(np.ravel_multi_index(to, sizes))))
    return lax.ppermute(x, axes, perm)


SMEM = pl.BlockSpec(memory_space=pltpu.SMEM)
INSIDE = pl.BlockSpec(memory_space=pltpu.VMEM)
ANY = pl.BlockSpec(memory_space=pl.ANY)


def call(kernel, ins, outs, in_specs=None, out_specs=None, scratch=(), limit=16, flops=0, moved_bytes=0):
    many = isinstance(outs, (list, tuple))
    return pl.pallas_call(
        kernel,
        in_specs=[SMEM, *(in_specs or [INSIDE] * (len(ins) - 1))],
        out_specs=out_specs or ([INSIDE] * len(outs) if many else INSIDE),
        out_shape=outs,
        scratch_shapes=list(scratch),
        cost_estimate=pl.CostEstimate(flops=flops, bytes_accessed=moved_bytes, transcendentals=0),
        compiler_params=pltpu.CompilerParams(vmem_limit_bytes=limit * 1024 * 1024),
    )(*ins)


def sds(shape, dtype):
    return jax.ShapeDtypeStruct(shape, dtype)


def softmax_over_coarse(rows, coarse, coarse_sq):
    logits = (lax.dot_general(coarse, rows, NT, preferred_element_type=F32) - 0.5 * coarse_sq) * inv_temper
    shifted = jnp.exp(logits - jnp.max(logits, axis=0, keepdims=True))
    return shifted / jnp.sum(shifted, axis=0, keepdims=True)


def prior_kernel(sc, fine, coarse, fine_sq, coarse_sq, prior):
    fine_sq[...] = jnp.sum(jnp.square(fine[...].astype(F32)), axis=1, keepdims=True)
    coarse_sq[...] = jnp.sum(jnp.square(coarse[...].astype(F32)), axis=1, keepdims=True)
    own = fine[pl.ds(pl.multiple_of(sc[S_K] * 128, 128), 128), :]
    parent = softmax_over_coarse(own, coarse[...], coarse_sq[...]).astype(BF16)
    prior[...] = lax.dot_general(parent, coarse[...], TN, preferred_element_type=F32)


def scores_kernel(sc, fine, fine_sq, *refs):
    n = len(refs) - 4
    pieces, (probs, peak, lse, rows) = refs[:n], refs[n:]
    for i in range(n):
        rows[128 * i : 128 * i + 128, :] = pieces[i][...]
    for b in range(n // 2):
        cols = slice(256 * b, 256 * b + 256)
        s = lax.dot_general(fine[...], rows[cols, :], NT, preferred_element_type=F32)
        s = (s - 0.5 * fine_sq[...]) * inv_temper
        top = jnp.max(s, axis=0, keepdims=True)
        p = jnp.exp(s - top)
        probs[:, cols] = p.astype(BF16)
        peak[:, cols] = top
        lse[:, cols] = top + jnp.log(jnp.sum(p, axis=0, keepdims=True))


def stats_kernel(sc, *refs):
    lses, (out,), (table,) = refs[: len(CHUNKS)], refs[len(CHUNKS) : -1], refs[-1:]
    at = 0
    for chunk, lse in zip(CHUNKS, lses):
        for i in range(len(chunk)):
            table[pl.ds(sc[S_P + at], 1), :] = lse[:, 128 * i : 128 * i + 128]
            at += 1
    for peer in range(NP):
        out[peer] = table[...]


def moment_kernel(sc, lse_all, *refs):
    nc = len(CHUNKS)
    probs, peaks, chunks = refs[:nc], refs[nc : 2 * nc], refs[2 * nc : 3 * nc]
    out, rows, resp, total, sems = refs[3 * nc :]
    copies, at = [], 0
    for i, chunk in enumerate(CHUNKS):
        n = 128 * len(chunk)
        copies.append(pltpu.make_async_copy(chunks[i], rows.at[pl.ds(at, n)], sems.at[i]))
        copies[-1].start()
        at += n
    top = jnp.max(lse_all[...], axis=0)
    total[...] = top + jnp.log(jnp.sum(jnp.exp(lse_all[...] - top[None]), axis=0))
    at = 0
    for chunk, prob, peak in zip(CHUNKS, probs, peaks):
        for i in range(len(chunk)):
            cols = slice(128 * i, 128 * i + 128)
            factor = jnp.exp(peak[:, cols] - total[pl.ds(sc[S_P + at], 1), :])
            resp[:, 128 * at : 128 * at + 128] = (prob[:, cols].astype(F32) * factor).astype(BF16)
            at += 1
    mass = lax.dot_general(jnp.ones((8, 128 * NP), BF16), resp[...], NT, preferred_element_type=F32)
    high = mass.astype(BF16).astype(F32)
    low = mass - high
    line = lax.broadcasted_iota(jnp.int32, (8, 128), 0)
    for j in range(8):
        cols = slice(128 * j, 128 * j + 128)
        both = jnp.where(line == 0, high[:, cols], jnp.where(line == 1, low[:, cols], 0.0))
        out[j, 128:136, :] = jnp.zeros((8, 1024), BF16)
        out[j, 128:136, 0:128] = both.astype(BF16)
    for copy in copies:
        copy.wait()
    for n in range(4):
        cols = slice(256 * n, 256 * n + 256)
        part = jnp.dot(resp[...], rows[:, cols], preferred_element_type=F32)
        for j in range(8):
            out[j, 0:128, cols] = part[128 * j : 128 * j + 128].astype(BF16)


def update_kernel(sc, *refs):
    blocks, prior, coarse, coarse_sq, low_out, keep, send, shares = refs
    moment = prior[...]
    mass = jnp.zeros((1, 128), F32)
    for j in range(8):
        moment = moment + blocks[j, 0:128, :].astype(F32)
        tail = blocks[j, 128:136, 0:128].astype(F32)
        mass = mass + tail[0:1] + tail[1:2]
    weight = mass + shrink
    diag = lax.broadcasted_iota(jnp.int32, (128, 128), 0) == lax.broadcasted_iota(jnp.int32, (128, 128), 1)
    column = jnp.sum(jnp.where(diag, jnp.broadcast_to(weight, (128, 128)), 0.0), axis=1, keepdims=True)
    low = (moment / column).astype(BF16)
    low_out[...] = low
    child = softmax_over_coarse(low, coarse[...], coarse_sq[...])
    shares[...] = (child * weight).astype(BF16)
    den = lax.dot_general(jnp.ones((8, 128), BF16), shares[...], NT, preferred_element_type=F32)[0:1]
    high = den.astype(BF16).astype(F32)
    rest = den - high
    line = lax.broadcasted_iota(jnp.int32, (8, 128), 0)
    dens = jnp.zeros((8, 128), F32)
    for q in range(4):
        cols = slice(128 * q, 128 * q + 128)
        dens = jnp.where(line == q, jnp.broadcast_to(high[:, cols], (8, 128)), dens)
        dens = jnp.where(line == q + 4, jnp.broadcast_to(rest[:, cols], (8, 128)), dens)
    for out, half in ((keep, sc[S_C]), (send, 1 - sc[S_C])):
        at = pl.multiple_of(half * 256, 256)
        num = jnp.dot(shares[pl.ds(at, 256), :], low, preferred_element_type=F32)
        for jr in range(8):
            for jc in range(8):
                out[jr * 8 + jc, 0:32, :] = num[32 * jr : 32 * jr + 32, 128 * jc : 128 * jc + 128].astype(out.dtype)
                out[jr * 8 + jc, 32:40, :] = dens.astype(out.dtype)


def coarse_kernel(sc, parts, coarse, out):
    total = jnp.sum(parts[...].astype(F32), axis=0)
    at = sc[S_C] * 256 + (sc[S_J] // 8) * 32
    col = sc[S_J] % 8
    dens = total[32:36] + total[36:40]
    line = lax.broadcasted_iota(jnp.int32, (4, 128), 0)
    row = jnp.sum(jnp.where(line == at // 128, dens, 0.0), axis=0, keepdims=True)
    r = lax.broadcasted_iota(jnp.int32, (32, 128), 0)
    lane = lax.broadcasted_iota(jnp.int32, (32, 128), 1)
    den = jnp.sum(jnp.where(lane == r + at % 128, jnp.broadcast_to(row, (32, 128)), 0.0), axis=1, keepdims=True)
    old = coarse[pl.ds(pl.multiple_of(at, 32), 32), pl.ds(pl.multiple_of(col * 128, 128), 128)]
    new = (total[0:32] + anchor * old.astype(F32)) / (den + anchor)
    out[...] = jnp.broadcast_to(new.astype(BF16)[None], (64, 32, 128))


def coarse_out_kernel(sc, mine, other, out, wide, sems):
    copies = []
    for i, (src, half) in enumerate(((mine, sc[S_C]), (other, 1 - sc[S_C]))):
        for jr in range(8):
            for jc in range(8):
                wide[256 * i + 32 * jr : 256 * i + 32 * jr + 32, 128 * jc : 128 * jc + 128] = src[jr * 8 + jc].astype(F32)
        to = out.at[pl.ds(pl.multiple_of(half * 256, 256), 256)]
        copies.append(pltpu.make_async_copy(wide.at[pl.ds(256 * i, 256)], to, sems.at[i]))
        copies[-1].start()
    for copy in copies:
        copy.wait()


def fine_out_kernel(sc, *refs):
    blocks, (out, wide, sems) = refs[:8], refs[8:]
    copies = []
    for j in range(8):
        wide[j] = blocks[j][...].astype(F32)
        to = out.at[pl.ds(pl.multiple_of(sc[S_K + j] * 128, 128), 128)]
        copies.append(pltpu.make_async_copy(wide.at[j], to, sems.at[j]))
        copies[-1].start()
    for copy in copies:
        copy.wait()


def scalar_table():
    yl, x, yh, z, c = (lax.axis_index(a) for a in ("yl", "x", "yh", "z", "c"))
    j = jnp.arange(8, dtype=jnp.int32)
    k = (yl ^ (j // 4)) * 4 + (x + j % 4) % 4
    dyh, dz, dc = (jnp.array(col, jnp.int32) for col in np.array(PIECES).T)
    p = ((yh ^ dyh) * 4 + (z - dz + 4) % 4) * 2 + (c ^ dc)
    i = jnp.arange(8, dtype=jnp.int32)
    tail = jnp.where(i == 0, c, ((yl * 4 + x) * 2 + yh) * 4 + z)
    return jnp.concatenate([k, p, tail]).astype(jnp.int32)


def step(embeds, fine, coarse):
    sc = scalar_table()

    def sent(x, axis, by):
        return moved(x, (axis,), (by,))

    up = sent(embeds, "z", 1)
    down = sent(embeds, "z", 3)
    across = sent(embeds, "yh", 1)
    across_up = sent(across, "z", 1)
    across_down = sent(across, "z", 3)
    far_up = sent(up, "z", 1)
    far_down = sent(across_down, "z", 3)

    def with_twin(*blocks):
        both = []
        for x in blocks:
            both += [x, sent(x, "c", 1)]
        return both

    fine_sq, coarse_sq, prior = call(
        prior_kernel, (sc, fine, coarse),
        [sds((1024, 1), F32), sds((512, 1), F32), sds((128, 1024), F32)],
        flops=300_000_000, moved_bytes=4_000_000,
    )

    inputs = (
        with_twin(embeds), with_twin(across), with_twin(up, down),
        with_twin(across_up, across_down), with_twin(far_up, far_down),
    )
    probs, peaks, lses, chunks = [], [], [], []
    for blocks in inputs:
        width = 128 * len(blocks)
        prob, peak, lse, rows = call(
            scores_kernel, (sc, fine, fine_sq, *blocks),
            [sds((1024, width), BF16), sds((1, width), F32), sds((1, width), F32), sds((width, 1024), BF16)],
            flops=2 * width * 1024 * 1024, moved_bytes=2_000_000 + width * 4096,
        )
        probs.append(prob)
        peaks.append(peak)
        lses.append(lse)
        chunks.append(rows)

    table = call(stats_kernel, (sc, *lses), sds((NP, NP, 128), F32), scratch=[VMEM((NP, 128), F32)])
    lse_all = lax.all_to_all(table, INNER, 0, 0, tiled=True)

    block = call(
        moment_kernel, (sc, lse_all, *probs, *peaks, *chunks),
        sds((8, ROWS_OUT, 1024), BF16),
        in_specs=[INSIDE] * (1 + 2 * len(CHUNKS)) + [ANY] * len(CHUNKS),
        scratch=[
            VMEM((128 * NP, 1024), BF16), VMEM((1024, 128 * NP), BF16), VMEM((NP, 128), F32),
            pltpu.SemaphoreType.DMA((len(CHUNKS),)),
        ],
        limit=24, flops=2 * 1024 * 2048 * 1024, moved_bytes=10_000_000,
    )
    mine = lax.all_to_all(block, GRP, 0, 0, tiled=True)

    low, keep, send = call(
        update_kernel, (sc, mine, prior, coarse, coarse_sq),
        [sds((128, 1024), BF16), sds((64, 40, 128), F32), sds((64, 40, 128), BF16)],
        scratch=[VMEM((512, 128), BF16)], flops=300_000_000, moved_bytes=6_000_000,
    )
    twin = moved(send, ("c",), (1,))
    lows = [low] + [sent(low, "x", 4 - d) for d in (1, 2, 3)]
    partner = sent(low, "yl", 1)
    lows += [partner] + [sent(partner, "x", 4 - d) for d in (1, 2, 3)]

    half = (keep + twin.astype(F32)).astype(BF16)
    parts = lax.all_to_all(half, CHIPS, 0, 0, tiled=True)
    new = call(coarse_kernel, (sc, parts, coarse), sds((64, 32, 128), BF16))
    mine_new = lax.all_to_all(new, CHIPS, 0, 0, tiled=True)
    other_new = moved(mine_new, ("c",), (1,))
    fine_update = call(
        fine_out_kernel, (sc, *lows), sds((1024, 1024), F32), out_specs=ANY,
        scratch=[VMEM((8, 128, 1024), F32), pltpu.SemaphoreType.DMA((8,))], limit=8,
        flops=1_000_000, moved_bytes=6_000_000,
    )
    coarse_update = call(
        coarse_out_kernel, (sc, mine_new, other_new), sds((512, 1024), F32), out_specs=ANY,
        scratch=[VMEM((512, 1024), F32), pltpu.SemaphoreType.DMA((2,))], limit=8,
    )
    return fine_update, coarse_update


def solution(mesh):
    finer = Mesh(mesh.devices.reshape(2, 4, 2, 4, 2), ("yl", "x", "yh", "z", "c"))
    return jax.shard_map(
        step,
        mesh=finer,
        in_specs=(P((*GRP, *INNER), None), P(INNER, None), P()),
        out_specs=(P(INNER, None), P()),
        check_vma=False,
    )
```

profile of v0, /device:TPU:1, one launch (start us, length us, event | category | flops | bytes accessed | tf_op | source)
XLA Modules:
  0.0 164.6 jit_solution(4069372160578717765)
XLA Ops:
  0.6 3.8 %collective-permute-start.1 = (bf16[128,1024]{1,0:T(8,128)(2,1)}, bf16[128,1024]{1,0:T(8,128)(2,1)S(1)}, u32[]{:S(2)}, u32[]{:S(2)}) collective-permute-start(bf16[128,1024]{1,0:T(8,128)(2,1)} %refs_0_.1), channel_id=1, source_target_pairs={{0,8},{8,0},{1,9},{9,1},{2,10},{10,2},{3,11},{11,3},{4,12},{12,4},... | collective-permute-start | bytes 786440 | tf_op jit(solution)/shard_map/ppermute | solution.py:43
  5.4 3.8 %collective-permute-start.5 = (bf16[128,1024]{1,0:T(8,128)(2,1)}, bf16[128,1024]{1,0:T(8,128)(2,1)S(1)}, u32[]{:S(2)}, u32[]{:S(2)}) collective-permute-start(bf16[128,1024]{1,0:T(8,128)(2,1)} %refs_0_.1), channel_id=1, source_target_pairs={{0,6},{2,0},{4,2},{6,4},{1,7},{3,1},{5,3},{7,5},{8,14},{10,8},{12,... | collective-permute-start | bytes 786440 | tf_op jit(solution)/shard_map/ppermute | solution.py:43
  10.4 3.7 %collective-permute-start.9 = (bf16[128,1024]{1,0:T(8,128)(2,1)S(1)}, bf16[128,1024]{1,0:T(8,128)(2,1)S(1)}, u32[]{:S(2)}, u32[]{:S(2)}) collective-permute-start(bf16[128,1024]{1,0:T(8,128)(2,1)S(1)} %collective-permute-done.1.refs_0_), channel_id=1, source_target_pairs={{0,6},{2,0},{4,2},{6,4},{1,7},{3,1},{5,3},{7,5},{8,14},{10,8},{12,... | collective-permute-start | bytes 786440 | tf_op jit(solution)/shard_map/ppermute | solution.py:43
  19.9 3.4 %collective-permute-start.13 = (bf16[128,1024]{1,0:T(8,128)(2,1)S(1)}, bf16[128,1024]{1,0:T(8,128)(2,1)S(1)}, u32[]{:S(2)}, u32[]{:S(2)}) collective-permute-start(bf16[128,1024]{1,0:T(8,128)(2,1)S(1)} %collective-permute-done.9.refs_2_), channel_id=1, source_target_pairs={{0,6},{2,0},{4,2},{6,4},{1,7},{3,1},{5,3},{7,5},{8,14},{10,8},{12,... | collective-permute-start | bytes 786440 | tf_op jit(solution)/shard_map/ppermute | solution.py:43
  24.0 2.3 %collective-permute-start.4 = (bf16[128,1024]{1,0:T(8,128)(2,1)S(1)}, bf16[128,1024]{1,0:T(8,128)(2,1)S(1)}, u32[]{:S(2)}, u32[]{:S(2)}) collective-permute-start(bf16[128,1024]{1,0:T(8,128)(2,1)S(1)} %collective-permute-done.3.refs_0_), channel_id=1, source_target_pairs={{0,1},{1,0},{2,3},{3,2},{4,5},{5,4},{6,7},{7,6},{8,9},{9,8},{10,11... | collective-permute-start | bytes 786440 | tf_op jit(solution)/shard_map/ppermute | solution.py:43
  29.9 1.9 %shard_map.77 = (f32[1024,1]{1,0:T(8,128)S(1)}, f32[512,1]{1,0:T(8,128)S(1)}, f32[128,1024]{1,0:T(8,128)S(1)}) custom-call(s32[32]{0:T(128)S(1)} %pad_add_fusion.sc, bf16[1024,1024]{1,0:T(8,128)(2,1)S(1)} %copy-done, bf16[512,1024]{1,0:T(8,128)(2,1)S(1)} %copy-done.1), custom_call_target="tpu_custom_call" | custom-call | flops 300000000 | bytes 4000000 | tf_op jit(solution)/shard_map/pallas_call | solution.py:53
  35.6 2.4 %shard_map.80 = (bf16[1024,512]{1,0:T(8,128)(2,1)S(1)}, f32[1,512]{1,0:T(1,128)S(1)}, f32[1,512]{1,0:T(1,128)S(1)}, bf16[512,1024]{1,0:T(8,128)(2,1)S(1)}) custom-call(s32[32]{0:T(128)S(1)} %pad_add_fusion.sc, bf16[1024,1024]{1,0:T(8,128)(2,1)S(1)} %copy-done, f32[1024,1]{1,0:T(8,128)S(1)} %get-tuple-element.28.fine_sq, ...), custom_call_target="tpu_custom_call" | custom-call | flops 1073741824 | bytes 4097152 | tf_op jit(solution)/shard_map/pallas_call | solution.py:53
  38.0 2.4 %shard_map.81 = (bf16[1024,512]{1,0:T(8,128)(2,1)S(1)}, f32[1,512]{1,0:T(1,128)S(1)}, f32[1,512]{1,0:T(1,128)S(1)}, bf16[512,1024]{1,0:T(8,128)(2,1)S(1)}) custom-call(s32[32]{0:T(128)S(1)} %pad_add_fusion.sc, bf16[1024,1024]{1,0:T(8,128)(2,1)S(1)} %copy-done, f32[1024,1]{1,0:T(8,128)S(1)} %get-tuple-element.28.fine_sq, ...), custom_call_target="tpu_custom_call" | custom-call | flops 1073741824 | bytes 4097152 | tf_op jit(solution)/shard_map/pallas_call | solution.py:53
  40.4 2.4 %shard_map.82 = (bf16[1024,512]{1,0:T(8,128)(2,1)S(1)}, f32[1,512]{1,0:T(1,128)S(1)}, f32[1,512]{1,0:T(1,128)S(1)}, bf16[512,1024]{1,0:T(8,128)(2,1)S(1)}) custom-call(s32[32]{0:T(128)S(1)} %pad_add_fusion.sc, bf16[1024,1024]{1,0:T(8,128)(2,1)S(1)} %copy-done, f32[1024,1]{1,0:T(8,128)S(1)} %get-tuple-element.28.fine_sq, ...), custom_call_target="tpu_custom_call" | custom-call | flops 1073741824 | bytes 4097152 | tf_op jit(solution)/shard_map/pallas_call | solution.py:53
  43.3 12.1 %all_to_all.20.lse_all = f32[16,16,128]{2,1,0:T(8,128)S(1)} all-to-all(f32[16,16,128]{2,1,0:T(8,128)S(1)} %shard_map.83), channel_id=1, replica_groups=mesh['yl'=2,'x'=4,'yh'=2,'z'=4,'c'=2] {'yh','z','c'}, dimensions={0} | all-to-all | bytes 262144 | tf_op jit(solution)/shard_map/all_to_all | solution.py:274
  55.5 6.8 %shard_map.84 = bf16[8,136,1024]{2,1,0:T(8,128)(2,1)S(1)} custom-call(s32[32]{0:T(128)S(1)} %pad_add_fusion.sc, f32[16,16,128]{2,1,0:T(8,128)S(1)} %all_to_all.20.lse_all, bf16[1024,256]{1,0:T(8,128)(2,1)S(1)} %get-tuple-element.34.refs_0_, bf16[1024,256]{1,0:T(8,128)(2,1)S(1)} %get-tuple-element.35.refs_1_, ...), custom_call_target="tpu_custom_call" | custom-call | flops 4294967296 | bytes 10000000 | tf_op jit(solution)/shard_map/pallas_call | solution.py:53
  62.3 31.7 %all_to_all.21.refs_0_ = bf16[8,136,1024]{2,1,0:T(8,128)(2,1)S(1)} all-to-all(bf16[8,136,1024]{2,1,0:T(8,128)(2,1)S(1)} %shard_map.84), channel_id=1, replica_groups=mesh['yl'=2,'x'=4,'yh'=2,'z'=4,'c'=2] {'yl','x'}, dimensions={0} | all-to-all | bytes 4456448 | tf_op jit(solution)/shard_map/all_to_all | solution.py:286
  94.0 2.2 %shard_map.85 = (bf16[128,1024]{1,0:T(8,128)(2,1)S(1)}, f32[64,40,128]{2,1,0:T(8,128)S(1)}, bf16[64,40,128]{2,1,0:T(8,128)(2,1)S(1)}) custom-call(s32[32]{0:T(128)S(1)} %pad_add_fusion.sc, bf16[8,136,1024]{2,1,0:T(8,128)(2,1)S(1)} %all_to_all.21.refs_0_, f32[128,1024]{1,0:T(8,128)S(1)} %get-tuple-element.49.refs_1_, bf16[512,1024]{1,0:T(8,128)(2,1)S(1)} %copy-done.2, ...), custom_call_target="tpu_custom_call" | custom-call | flops 300000000 | bytes 6000000 | tf_op jit(solution)/shard_map/pallas_call | solution.py:53
  96.2 2.1 %collective-permute-start.22 = (bf16[64,40,128]{2,1,0:T(8,128)(2,1)S(1)}, bf16[64,40,128]{2,1,0:T(8,128)(2,1)S(1)}, u32[]{:S(2)}, u32[]{:S(2)}) collective-permute-start(bf16[64,40,128]{2,1,0:T(8,128)(2,1)S(1)} %get-tuple-element.53), channel_id=1, source_target_pairs={{0,1},{1,0},{2,3},{3,2},{4,5},{5,4},{6,7},{7,6},{8,9},{9,8},{10,11... | collective-permute-start | bytes 1966088 | tf_op jit(solution)/shard_map/ppermute | solution.py:43
  100.3 17.2 %all_to_all.22.parts = bf16[64,40,128]{2,1,0:T(8,128)(2,1)S(1)} all-to-all(bf16[64,40,128]{2,1,0:T(8,128)(2,1)S(1)} %add_convert_fusion), channel_id=1, replica_groups=mesh['yl'=2,'x'=4,'yh'=2,'z'=4,'c'=2] {'yl','x','yh','z'}, dimensions={0} | all-to-all | bytes 1310720 | tf_op jit(solution)/shard_map/all_to_all | solution.py:299
  119.0 5.5 %all-to-all-start.3 = ((bf16[64,32,128]{2,1,0:T(8,128)(2,1)}), bf16[64,32,128]{2,1,0:T(8,128)(2,1)S(1)}, u32[]{:S(2)}, u32[]{:S(2)}) async-start(bf16[64,32,128]{2,1,0:T(8,128)(2,1)} %shard_map.87), calls=%async_computation.3 | async-start | bytes 1048576 | tf_op jit(solution)/shard_map/all_to_all | solution.py:301
  127.0 2.5 %collective-permute-start.16 = (bf16[128,1024]{1,0:T(8,128)(2,1)S(1)}, bf16[128,1024]{1,0:T(8,128)(2,1)S(1)}, u32[]{:S(2)}, u32[]{:S(2)}) collective-permute-start(bf16[128,1024]{1,0:T(8,128)(2,1)S(1)} %get-tuple-element.51.refs_0_), channel_id=1, source_target_pairs={{0,32},{16,48},{32,0},{48,16},{1,33},{17,49},{33,1},{49,17},{2,34}... | collective-permute-start | bytes 786440 | tf_op jit(solution)/shard_map/ppermute | solution.py:43
  129.5 5.7 %all-to-all-done.3.mine = bf16[64,32,128]{2,1,0:T(8,128)(2,1)S(1)} async-done(((bf16[64,32,128]{2,1,0:T(8,128)(2,1)}), bf16[64,32,128]{2,1,0:T(8,128)(2,1)S(1)}, u32[]{:S(2)}, u32[]{:S(2)}) %all-to-all-start.3) | async-done | bytes 524320 | tf_op jit(solution)/shard_map/all_to_all | solution.py:301
  135.3 5.4 %collective-permute-start.23 = (bf16[64,32,128]{2,1,0:T(8,128)(2,1)S(1)}, bf16[64,32,128]{2,1,0:T(8,128)(2,1)S(1)}, u32[]{:S(2)}, u32[]{:S(2)}) collective-permute-start(bf16[64,32,128]{2,1,0:T(8,128)(2,1)S(1)} %all-to-all-done.3.mine), channel_id=1, source_target_pairs={{0,1},{1,0},{2,3},{3,2},{4,5},{5,4},{6,7},{7,6},{8,9},{9,8},{10,11... | collective-permute-start | bytes 1572872 | tf_op jit(solution)/shard_map/ppermute | solution.py:43
  144.6 3.9 %collective-permute-done.15.refs_1_ = bf16[128,1024]{1,0:T(8,128)(2,1)S(1)} collective-permute-done((bf16[128,1024]{1,0:T(8,128)(2,1)S(1)}, bf16[128,1024]{1,0:T(8,128)(2,1)S(1)}, u32[]{:S(2)}, u32[]{:S(2)}) %collective-permute-start.15) | collective-permute-done | bytes 262176 | tf_op jit(solution)/shard_map/ppermute | solution.py:43
  148.5 2.4 %collective-permute-done.21.refs_7_ = bf16[128,1024]{1,0:T(8,128)(2,1)S(1)} collective-permute-done((bf16[128,1024]{1,0:T(8,128)(2,1)S(1)}, bf16[128,1024]{1,0:T(8,128)(2,1)S(1)}, u32[]{:S(2)}, u32[]{:S(2)}) %collective-permute-start.21) | collective-permute-done | bytes 262176 | tf_op jit(solution)/shard_map/ppermute | solution.py:43
  150.9 4.8 %collective-permute-done.20.refs_6_ = bf16[128,1024]{1,0:T(8,128)(2,1)S(1)} collective-permute-done((bf16[128,1024]{1,0:T(8,128)(2,1)S(1)}, bf16[128,1024]{1,0:T(8,128)(2,1)S(1)}, u32[]{:S(2)}, u32[]{:S(2)}) %collective-permute-start.20) | collective-permute-done | bytes 262176 | tf_op jit(solution)/shard_map/ppermute | solution.py:43
  155.7 4.1 %collective-permute-done.19.refs_5_ = bf16[128,1024]{1,0:T(8,128)(2,1)S(1)} collective-permute-done((bf16[128,1024]{1,0:T(8,128)(2,1)S(1)}, bf16[128,1024]{1,0:T(8,128)(2,1)S(1)}, u32[]{:S(2)}, u32[]{:S(2)}) %collective-permute-start.19) | collective-permute-done | bytes 262176 | tf_op jit(solution)/shard_map/ppermute | solution.py:43
  159.8 2.6 %shard_map.86 = f32[1024,1024]{1,0:T(8,128)} custom-call(s32[32]{0:T(128)S(1)} %pad_add_fusion.sc, bf16[128,1024]{1,0:T(8,128)(2,1)S(1)} %get-tuple-element.51.refs_0_, bf16[128,1024]{1,0:T(8,128)(2,1)S(1)} %collective-permute-done.15.refs_1_, bf16[128,1024]{1,0:T(8,128)(2,1)S(1)} %collective-permute-done.16.refs_2_, ...), custom_call_target="tpu_custom_call" | custom-call | flops 1000000 | bytes 6000000 | tf_op jit(solution)/shard_map/pallas_call | solution.py:53
  (53 shorter events, 28.2 us)
Async XLA Ops:
  0.6 9.8 %collective-permute-start.1 = (bf16[128,1024]{1,0:T(8,128)(2,1)}, bf16[128,1024]{1,0:T(8,128)(2,1)S(1)}, u32[]{:S(2)}, u32[]{:S(2)}) collective-permute-start(bf16[128,1024]{1,0:T(8,128)(2,1)} %refs_0_.1), channel_id=1, source_target_pairs={{0,8},{8,0},{1,9},{9,1},{2,10},{10,2},{3,11},{11,3},{4,12},{12,4},... | collective-permute-start | bytes 786440 | tf_op jit(solution)/shard_map/ppermute | solution.py:43
  4.4 9.8 %collective-permute-start = (bf16[128,1024]{1,0:T(8,128)(2,1)}, bf16[128,1024]{1,0:T(8,128)(2,1)S(1)}, u32[]{:S(2)}, u32[]{:S(2)}) collective-permute-start(bf16[128,1024]{1,0:T(8,128)(2,1)} %refs_0_.1), channel_id=1, source_target_pairs={{0,1},{1,0},{2,3},{3,2},{4,5},{5,4},{6,7},{7,6},{8,9},{9,8},{10,11... | collective-permute-start | bytes 786440 | tf_op jit(solution)/shard_map/ppermute | solution.py:43
  5.4 10.6 %collective-permute-start.5 = (bf16[128,1024]{1,0:T(8,128)(2,1)}, bf16[128,1024]{1,0:T(8,128)(2,1)S(1)}, u32[]{:S(2)}, u32[]{:S(2)}) collective-permute-start(bf16[128,1024]{1,0:T(8,128)(2,1)} %refs_0_.1), channel_id=1, source_target_pairs={{0,6},{2,0},{4,2},{6,4},{1,7},{3,1},{5,3},{7,5},{8,14},{10,8},{12,... | collective-permute-start | bytes 786440 | tf_op jit(solution)/shard_map/ppermute | solution.py:43
  9.2 9.0 %collective-permute-start.3 = (bf16[128,1024]{1,0:T(8,128)(2,1)}, bf16[128,1024]{1,0:T(8,128)(2,1)S(1)}, u32[]{:S(2)}, u32[]{:S(2)}) collective-permute-start(bf16[128,1024]{1,0:T(8,128)(2,1)} %refs_0_.1), channel_id=1, source_target_pairs={{0,2},{2,4},{4,6},{6,0},{1,3},{3,5},{5,7},{7,1},{8,10},{10,12},{12... | collective-permute-start | bytes 786440 | tf_op jit(solution)/shard_map/ppermute | solution.py:43
  10.4 9.5 %collective-permute-start.9 = (bf16[128,1024]{1,0:T(8,128)(2,1)S(1)}, bf16[128,1024]{1,0:T(8,128)(2,1)S(1)}, u32[]{:S(2)}, u32[]{:S(2)}) collective-permute-start(bf16[128,1024]{1,0:T(8,128)(2,1)S(1)} %collective-permute-done.1.refs_0_), channel_id=1, source_target_pairs={{0,6},{2,0},{4,2},{6,4},{1,7},{3,1},{5,3},{7,5},{8,14},{10,8},{12,... | collective-permute-start | bytes 786440 | tf_op jit(solution)/shard_map/ppermute | solution.py:43
  14.2 9.8 %collective-permute-start.7 = (bf16[128,1024]{1,0:T(8,128)(2,1)S(1)}, bf16[128,1024]{1,0:T(8,128)(2,1)S(1)}, u32[]{:S(2)}, u32[]{:S(2)}) collective-permute-start(bf16[128,1024]{1,0:T(8,128)(2,1)S(1)} %collective-permute-done.1.refs_0_), channel_id=1, source_target_pairs={{0,2},{2,4},{4,6},{6,0},{1,3},{3,5},{5,7},{7,1},{8,10},{10,12},{12... | collective-permute-start | bytes 786440 | tf_op jit(solution)/shard_map/ppermute | solution.py:43
  14.2 12.2 %collective-permute-start.2 = (bf16[128,1024]{1,0:T(8,128)(2,1)S(1)}, bf16[128,1024]{1,0:T(8,128)(2,1)S(1)}, u32[]{:S(2)}, u32[]{:S(2)}) collective-permute-start(bf16[128,1024]{1,0:T(8,128)(2,1)S(1)} %collective-permute-done.1.refs_0_), channel_id=1, source_target_pairs={{0,1},{1,0},{2,3},{3,2},{4,5},{5,4},{6,7},{7,6},{8,9},{9,8},{10,11... | collective-permute-start | bytes 786440 | tf_op jit(solution)/shard_map/ppermute | solution.py:43
  16.0 10.5 %collective-permute-start.6 = (bf16[128,1024]{1,0:T(8,128)(2,1)S(1)}, bf16[128,1024]{1,0:T(8,128)(2,1)S(1)}, u32[]{:S(2)}, u32[]{:S(2)}) collective-permute-start(bf16[128,1024]{1,0:T(8,128)(2,1)S(1)} %collective-permute-done.5.refs_2_), channel_id=1, source_target_pairs={{0,1},{1,0},{2,3},{3,2},{4,5},{5,4},{6,7},{7,6},{8,9},{9,8},{10,11... | collective-permute-start | bytes 786440 | tf_op jit(solution)/shard_map/ppermute | solution.py:43
  18.2 13.7 %collective-permute-start.11 = (bf16[128,1024]{1,0:T(8,128)(2,1)S(1)}, bf16[128,1024]{1,0:T(8,128)(2,1)S(1)}, u32[]{:S(2)}, u32[]{:S(2)}) collective-permute-start(bf16[128,1024]{1,0:T(8,128)(2,1)S(1)} %collective-permute-done.3.refs_0_), channel_id=1, source_target_pairs={{0,2},{2,4},{4,6},{6,0},{1,3},{3,5},{5,7},{7,1},{8,10},{10,12},{12... | collective-permute-start | bytes 786440 | tf_op jit(solution)/shard_map/ppermute | solution.py:43
  19.9 12.1 %collective-permute-start.13 = (bf16[128,1024]{1,0:T(8,128)(2,1)S(1)}, bf16[128,1024]{1,0:T(8,128)(2,1)S(1)}, u32[]{:S(2)}, u32[]{:S(2)}) collective-permute-start(bf16[128,1024]{1,0:T(8,128)(2,1)S(1)} %collective-permute-done.9.refs_2_), channel_id=1, source_target_pairs={{0,6},{2,0},{4,2},{6,4},{1,7},{3,1},{5,3},{7,5},{8,14},{10,8},{12,... | collective-permute-start | bytes 786440 | tf_op jit(solution)/shard_map/ppermute | solution.py:43
  24.0 11.6 %collective-permute-start.4 = (bf16[128,1024]{1,0:T(8,128)(2,1)S(1)}, bf16[128,1024]{1,0:T(8,128)(2,1)S(1)}, u32[]{:S(2)}, u32[]{:S(2)}) collective-permute-start(bf16[128,1024]{1,0:T(8,128)(2,1)S(1)} %collective-permute-done.3.refs_0_), channel_id=1, source_target_pairs={{0,1},{1,0},{2,3},{3,2},{4,5},{5,4},{6,7},{7,6},{8,9},{9,8},{10,11... | collective-permute-start | bytes 786440 | tf_op jit(solution)/shard_map/ppermute | solution.py:43
  26.4 11.6 %collective-permute-start.10 = (bf16[128,1024]{1,0:T(8,128)(2,1)S(1)}, bf16[128,1024]{1,0:T(8,128)(2,1)S(1)}, u32[]{:S(2)}, u32[]{:S(2)}) collective-permute-start(bf16[128,1024]{1,0:T(8,128)(2,1)S(1)} %collective-permute-done.9.refs_2_), channel_id=1, source_target_pairs={{0,1},{1,0},{2,3},{3,2},{4,5},{5,4},{6,7},{7,6},{8,9},{9,8},{10,11... | collective-permute-start | bytes 786440 | tf_op jit(solution)/shard_map/ppermute | solution.py:43
  26.5 11.5 %collective-permute-start.8 = (bf16[128,1024]{1,0:T(8,128)(2,1)S(1)}, bf16[128,1024]{1,0:T(8,128)(2,1)S(1)}, u32[]{:S(2)}, u32[]{:S(2)}) collective-permute-start(bf16[128,1024]{1,0:T(8,128)(2,1)S(1)} %collective-permute-done.7.refs_0_), channel_id=1, source_target_pairs={{0,1},{1,0},{2,3},{3,2},{4,5},{5,4},{6,7},{7,6},{8,9},{9,8},{10,11... | collective-permute-start | bytes 786440 | tf_op jit(solution)/shard_map/ppermute | solution.py:43
  31.9 8.5 %collective-permute-start.12 = (bf16[128,1024]{1,0:T(8,128)(2,1)S(1)}, bf16[128,1024]{1,0:T(8,128)(2,1)S(1)}, u32[]{:S(2)}, u32[]{:S(2)}) collective-permute-start(bf16[128,1024]{1,0:T(8,128)(2,1)S(1)} %collective-permute-done.11.refs_0_), channel_id=1, source_target_pairs={{0,1},{1,0},{2,3},{3,2},{4,5},{5,4},{6,7},{7,6},{8,9},{9,8},{10,11... | collective-permute-start | bytes 786440 | tf_op jit(solution)/shard_map/ppermute | solution.py:43
  32.0 8.4 %collective-permute-start.14 = (bf16[128,1024]{1,0:T(8,128)(2,1)S(1)}, bf16[128,1024]{1,0:T(8,128)(2,1)S(1)}, u32[]{:S(2)}, u32[]{:S(2)}) collective-permute-start(bf16[128,1024]{1,0:T(8,128)(2,1)S(1)} %collective-permute-done.13.refs_2_), channel_id=1, source_target_pairs={{0,1},{1,0},{2,3},{3,2},{4,5},{5,4},{6,7},{7,6},{8,9},{9,8},{10,11... | collective-permute-start | bytes 786440 | tf_op jit(solution)/shard_map/ppermute | solution.py:43
  119.0 16.2 %all-to-all-start.3 = ((bf16[64,32,128]{2,1,0:T(8,128)(2,1)}), bf16[64,32,128]{2,1,0:T(8,128)(2,1)S(1)}, u32[]{:S(2)}, u32[]{:S(2)}) async-start(bf16[64,32,128]{2,1,0:T(8,128)(2,1)} %shard_map.87), calls=%async_computation.3 | async-start | bytes 1048576 | tf_op jit(solution)/shard_map/all_to_all | solution.py:301
  124.6 16.3 %collective-permute-start.18 = (bf16[128,1024]{1,0:T(8,128)(2,1)S(1)}, bf16[128,1024]{1,0:T(8,128)(2,1)S(1)}, u32[]{:S(2)}, u32[]{:S(2)}) collective-permute-start(bf16[128,1024]{1,0:T(8,128)(2,1)S(1)} %get-tuple-element.51.refs_0_), channel_id=1, source_target_pairs={{0,64},{64,0},{1,65},{65,1},{2,66},{66,2},{3,67},{67,3},{4,68},{68... | collective-permute-start | bytes 786440 | tf_op jit(solution)/shard_map/ppermute | solution.py:43
  125.8 16.4 %collective-permute-start.17 = (bf16[128,1024]{1,0:T(8,128)(2,1)S(1)}, bf16[128,1024]{1,0:T(8,128)(2,1)S(1)}, u32[]{:S(2)}, u32[]{:S(2)}) collective-permute-start(bf16[128,1024]{1,0:T(8,128)(2,1)S(1)} %get-tuple-element.51.refs_0_), channel_id=1, source_target_pairs={{0,16},{16,32},{32,48},{48,0},{1,17},{17,33},{33,49},{49,1},{2,18}... | collective-permute-start | bytes 786440 | tf_op jit(solution)/shard_map/ppermute | solution.py:43
  127.0 16.2 %collective-permute-start.16 = (bf16[128,1024]{1,0:T(8,128)(2,1)S(1)}, bf16[128,1024]{1,0:T(8,128)(2,1)S(1)}, u32[]{:S(2)}, u32[]{:S(2)}) collective-permute-start(bf16[128,1024]{1,0:T(8,128)(2,1)S(1)} %get-tuple-element.51.refs_0_), channel_id=1, source_target_pairs={{0,32},{16,48},{32,0},{48,16},{1,33},{17,49},{33,1},{49,17},{2,34}... | collective-permute-start | bytes 786440 | tf_op jit(solution)/shard_map/ppermute | solution.py:43
  135.3 27.2 %collective-permute-start.23 = (bf16[64,32,128]{2,1,0:T(8,128)(2,1)S(1)}, bf16[64,32,128]{2,1,0:T(8,128)(2,1)S(1)}, u32[]{:S(2)}, u32[]{:S(2)}) collective-permute-start(bf16[64,32,128]{2,1,0:T(8,128)(2,1)S(1)} %all-to-all-done.3.mine), channel_id=1, source_target_pairs={{0,1},{1,0},{2,3},{3,2},{4,5},{5,4},{6,7},{7,6},{8,9},{9,8},{10,11... | collective-permute-start | bytes 1572872 | tf_op jit(solution)/shard_map/ppermute | solution.py:43
  140.7 7.9 %collective-permute-start.15 = (bf16[128,1024]{1,0:T(8,128)(2,1)S(1)}, bf16[128,1024]{1,0:T(8,128)(2,1)S(1)}, u32[]{:S(2)}, u32[]{:S(2)}) collective-permute-start(bf16[128,1024]{1,0:T(8,128)(2,1)S(1)} %get-tuple-element.51.refs_0_), channel_id=1, source_target_pairs={{0,48},{16,0},{32,16},{48,32},{1,49},{17,1},{33,17},{49,33},{2,50}... | collective-permute-start | bytes 786440 | tf_op jit(solution)/shard_map/ppermute | solution.py:43
  140.9 10.0 %collective-permute-start.21 = (bf16[128,1024]{1,0:T(8,128)(2,1)S(1)}, bf16[128,1024]{1,0:T(8,128)(2,1)S(1)}, u32[]{:S(2)}, u32[]{:S(2)}) collective-permute-start(bf16[128,1024]{1,0:T(8,128)(2,1)S(1)} %collective-permute-done.18.refs_4_), channel_id=1, source_target_pairs={{0,16},{16,32},{32,48},{48,0},{1,17},{17,33},{33,49},{49,1},{2,18}... | collective-permute-start | bytes 786440 | tf_op jit(solution)/shard_map/ppermute | solution.py:43
  142.2 13.6 %collective-permute-start.20 = (bf16[128,1024]{1,0:T(8,128)(2,1)S(1)}, bf16[128,1024]{1,0:T(8,128)(2,1)S(1)}, u32[]{:S(2)}, u32[]{:S(2)}) collective-permute-start(bf16[128,1024]{1,0:T(8,128)(2,1)S(1)} %collective-permute-done.18.refs_4_), channel_id=1, source_target_pairs={{0,32},{16,48},{32,0},{48,16},{1,33},{17,49},{33,1},{49,17},{2,34}... | collective-permute-start | bytes 786440 | tf_op jit(solution)/shard_map/ppermute | solution.py:43
  143.2 16.6 %collective-permute-start.19 = (bf16[128,1024]{1,0:T(8,128)(2,1)S(1)}, bf16[128,1024]{1,0:T(8,128)(2,1)S(1)}, u32[]{:S(2)}, u32[]{:S(2)}) collective-permute-start(bf16[128,1024]{1,0:T(8,128)(2,1)S(1)} %collective-permute-done.18.refs_4_), channel_id=1, source_target_pairs={{0,48},{16,0},{32,16},{48,32},{1,49},{17,1},{33,17},{49,33},{2,50}... | collective-permute-start | bytes 786440 | tf_op jit(solution)/shard_map/ppermute | solution.py:43
  (5 other events, 41.0 us)
where the time goes:
time: 165 us
  blocking collectives  61.1 us (37%)
  starting transfers between devices  43.4 us (26%)
  Pallas kernels  27.9 us (17%)
  waiting for transfers between devices  27.4 us (17%)
  local copies, waits for them, and re-layouts  2.83 us (2%)
    ppermute x24, starting transfers between devices, moved(): return lax.ppermute(x, axes, perm)  37.9 us
    all_to_all x1, blocking collectives, step(): mine = lax.all_to_all(block, GRP, 0, 0, tiled=True)  31.7 us
    pallas_call x12, Pallas kernels, call(): pl.pallas_call(kernel, in_specs=[SMEM, *(in_specs or [INSIDE] * (len(ins)...  27.9 us
    ppermute x24, waiting for transfers between devices, moved(): return lax.ppermute(x, axes, perm)  21.7 us
    all_to_all x1, blocking collectives, step(): parts = lax.all_to_all(half, CHIPS, 0, 0, tiled=True)  17.2 us
    all_to_all x1, blocking collectives, step(): lse_all = lax.all_to_all(table, INNER, 0, 0, tiled=True)  12.1 us
    all_to_all x1, waiting for transfers between devices, step(): mine_new = lax.all_to_all(new, CHIPS, 0, 0, tiled=True)  5.75 us
    all_to_all x1, starting transfers between devices, step(): mine_new = lax.all_to_all(new, CHIPS, 0, 0, tiled=True)  5.54 us
  transfers between devices with their start and end apart: 25, of which 9 were waited for; matrix products, arithmetic and copies ran while one was open for 0% of the time, Pallas kernels for 8%

commit v1 on v0

--- a/solution.py
+++ b/solution.py
@@ -1,3 +1,5 @@
+import functools
+
 import numpy as np
 import jax
 import jax.numpy as jnp
@@ -17,7 +19,6 @@
 shrink = 1.0
 anchor = 8.0
 inv_temper = 50.0
-ROWS_OUT = 136
 NT = (((1,), (1,)), ((), ()))
 TN = (((0,), (0,)), ((), ()))
 VMEM = pltpu.VMEM
@@ -48,7 +49,7 @@
 ANY = pl.BlockSpec(memory_space=pl.ANY)
 
 
-def call(kernel, ins, outs, in_specs=None, out_specs=None, scratch=(), limit=16, flops=0, moved_bytes=0):
+def call(kernel, ins, outs, in_specs=None, out_specs=None, scratch=(), limit=16, aliases=None, flops=0, moved_bytes=0):
     many = isinstance(outs, (list, tuple))
     return pl.pallas_call(
         kernel,
@@ -56,6 +57,7 @@
         out_specs=out_specs or ([INSIDE] * len(outs) if many else INSIDE),
         out_shape=outs,
         scratch_shapes=list(scratch),
+        input_output_aliases=aliases or {},
         cost_estimate=pl.CostEstimate(flops=flops, bytes_accessed=moved_bytes, transcendentals=0),
         compiler_params=pltpu.CompilerParams(vmem_limit_bytes=limit * 1024 * 1024),
     )(*ins)
@@ -106,10 +108,23 @@
         out[peer] = table[...]
 
 
-def moment_kernel(sc, lse_all, *refs):
+def responsibilities(sc, first, probs, peaks, total, resp):
+    at = 0
+    for chunk, prob, peak in zip(CHUNKS, probs, peaks):
+        for i in range(len(chunk)):
+            cols = slice(128 * i, 128 * i + 128)
+            factor = jnp.exp(peak[:, cols] - total[pl.ds(sc[S_P + at], 1), :])
+            for j in range(4):
+                k = pl.multiple_of(sc[S_K + first + j] * 128, 128)
+                part = prob[pl.ds(k, 128), cols].astype(F32) * factor
+                resp[128 * j : 128 * j + 128, 128 * at : 128 * at + 128] = part.astype(BF16)
+            at += 1
+
+
+def moment_far_kernel(sc, lse_all, *refs):
     nc = len(CHUNKS)
     probs, peaks, chunks = refs[:nc], refs[nc : 2 * nc], refs[2 * nc : 3 * nc]
-    out, rows, resp, total, sems = refs[3 * nc :]
+    out, resp, rows, total, sems = refs[3 * nc :]
     copies, at = [], 0
     for i, chunk in enumerate(CHUNKS):
         n = 128 * len(chunk)
@@ -118,39 +133,66 @@
         at += n
     top = jnp.max(lse_all[...], axis=0)
     total[...] = top + jnp.log(jnp.sum(jnp.exp(lse_all[...] - top[None]), axis=0))
-    at = 0
-    for chunk, prob, peak in zip(CHUNKS, probs, peaks):
-        for i in range(len(chunk)):
-            cols = slice(128 * i, 128 * i + 128)
-            factor = jnp.exp(peak[:, cols] - total[pl.ds(sc[S_P + at], 1), :])
-            resp[:, 128 * at : 128 * at + 128] = (prob[:, cols].astype(F32) * factor).astype(BF16)
-            at += 1
-    mass = lax.dot_general(jnp.ones((8, 128 * NP), BF16), resp[...], NT, preferred_element_type=F32)
-    high = mass.astype(BF16).astype(F32)
-    low = mass - high
-    line = lax.broadcasted_iota(jnp.int32, (8, 128), 0)
-    for j in range(8):
-        cols = slice(128 * j, 128 * j + 128)
-        both = jnp.where(line == 0, high[:, cols], jnp.where(line == 1, low[:, cols], 0.0))
-        out[j, 128:136, :] = jnp.zeros((8, 1024), BF16)
-        out[j, 128:136, 0:128] = both.astype(BF16)
+    responsibilities(sc, 4, probs, peaks, total, resp)
     for copy in copies:
         copy.wait()
-    for n in range(4):
+    for n in range(2):
+        part = jnp.dot(resp[...], rows[:, 512 + 256 * n : 768 + 256 * n], preferred_element_type=F32)
+        out[:, 256 * n : 256 * n + 256] = part.astype(BF16)
+
+
+def moment_a_kernel(sc, total, resp1, rows, *refs):
+    nc = len(CHUNKS)
+    probs, peaks, outs, resp0 = refs[:nc], refs[nc : 2 * nc], refs[2 * nc : 2 * nc + 4], refs[-1]
+    responsibilities(sc, 0, probs, peaks, total, resp0)
+    line = lax.broadcasted_iota(jnp.int32, (8, 128), 0)
+    for h, resp in ((1, resp1), (0, resp0)):
+        mass = lax.dot_general(jnp.ones((8, 128 * NP), BF16), resp[...], NT, preferred_element_type=F32)
+        high = mass.astype(BF16).astype(F32)
+        low = mass - high
+        for n in range(2):
+            cols = slice(256 * n, 256 * n + 256)
+            part = jnp.dot(resp[...], rows[:, cols], preferred_element_type=F32)
+            for j in range(4):
+                outs[j][h, 0:128, cols] = part[128 * j : 128 * j + 128].astype(outs[j].dtype)
+        for j in range(4):
+            cols = slice(128 * j, 128 * j + 128)
+            both = jnp.where(line == 0, high[:, cols], jnp.where(line == 1, low[:, cols], 0.0))
+            outs[j][h, 128:136, :] = jnp.zeros((8, 512), outs[j].dtype)
+            outs[j][h, 128:136, 0:128] = both.astype(outs[j].dtype)
+
+
+def moment_b_kernel(sc, resp0, rows, got, *outs):
+    for n in range(2):
         cols = slice(256 * n, 256 * n + 256)
-        part = jnp.dot(resp[...], rows[:, cols], preferred_element_type=F32)
-        for j in range(8):
-            out[j, 0:128, cols] = part[128 * j : 128 * j + 128].astype(BF16)
+        part = jnp.dot(resp0[...], rows[:, 512 + 256 * n : 768 + 256 * n], preferred_element_type=F32)
+        part = part + got[:, cols].astype(F32)
+        for j in range(4):
+            outs[j][:, cols] = part[128 * j : 128 * j + 128].astype(outs[j].dtype)
+
+
+def sum_a_kernel(sc, own, got1, got2, got3, keep, send):
+    sums = [own[h] + got1[h].astype(F32) + got2[h].astype(F32) + got3[h].astype(F32) for h in range(2)]
+    keep[...] = sums[0]
+    mass = sums[1][128:129] + sums[1][129:130]
+    high = mass.astype(BF16).astype(F32)
+    line = lax.broadcasted_iota(jnp.int32, (8, 512), 0)
+    both = jnp.where(line == 0, high, jnp.where(line == 1, mass - high, 0.0))
+    send[0:128, :] = sums[1][0:128].astype(BF16)
+    send[128:136, :] = both.astype(BF16)
 
 
 def update_kernel(sc, *refs):
-    blocks, prior, coarse, coarse_sq, low_out, keep, send, shares = refs
-    moment = prior[...]
-    mass = jnp.zeros((1, 128), F32)
-    for j in range(8):
-        moment = moment + blocks[j, 0:128, :].astype(F32)
-        tail = blocks[j, 128:136, 0:128].astype(F32)
-        mass = mass + tail[0:1] + tail[1:2]
+    keep_a, got_a, own_b, got_b, (prior, coarse, coarse_sq, low_out, keep, send, shares) = (
+        refs[0], refs[1], refs[2], refs[3:6], refs[6:],
+    )
+    left = prior[:, 0:512] + keep_a[0:128, :] + got_a[0:128, :].astype(F32)
+    right = prior[:, 512:1024] + own_b[...]
+    for got in got_b:
+        right = right + got[...].astype(F32)
+    moment = jnp.concatenate([left, right], axis=1)
+    tail = keep_a[128:136, 0:128] + got_a[128:136, 0:128].astype(F32)
+    mass = tail[0:1] + tail[1:2]
     weight = mass + shrink
     diag = lax.broadcasted_iota(jnp.int32, (128, 128), 0) == lax.broadcasted_iota(jnp.int32, (128, 128), 1)
     column = jnp.sum(jnp.where(diag, jnp.broadcast_to(weight, (128, 128)), 0.0), axis=1, keepdims=True)
@@ -191,25 +233,23 @@
     out[...] = jnp.broadcast_to(new.astype(BF16)[None], (64, 32, 128))
 
 
-def coarse_out_kernel(sc, mine, other, out, wide, sems):
+def coarse_out_kernel(flip, sc, src, *refs):
+    out, wide, sem = refs[-3:]
+    half = sc[S_C] + flip - 2 * flip * sc[S_C]
+    for jr in range(8):
+        for jc in range(8):
+            wide[32 * jr : 32 * jr + 32, 128 * jc : 128 * jc + 128] = src[jr * 8 + jc].astype(F32)
+    copy = pltpu.make_async_copy(wide, out.at[pl.ds(pl.multiple_of(half * 256, 256), 256)], sem)
+    copy.start()
+    copy.wait()
+
+
+def fine_out_kernel(first, sc, *refs):
+    blocks, (out, wide, sems) = refs[:4], refs[-3:]
     copies = []
-    for i, (src, half) in enumerate(((mine, sc[S_C]), (other, 1 - sc[S_C]))):
-        for jr in range(8):
-            for jc in range(8):
-                wide[256 * i + 32 * jr : 256 * i + 32 * jr + 32, 128 * jc : 128 * jc + 128] = src[jr * 8 + jc].astype(F32)
-        to = out.at[pl.ds(pl.multiple_of(half * 256, 256), 256)]
-        copies.append(pltpu.make_async_copy(wide.at[pl.ds(256 * i, 256)], to, sems.at[i]))
-        copies[-1].start()
-    for copy in copies:
-        copy.wait()
-
-
-def fine_out_kernel(sc, *refs):
-    blocks, (out, wide, sems) = refs[:8], refs[8:]
-    copies = []
-    for j in range(8):
+    for j in range(4):
         wide[j] = blocks[j][...].astype(F32)
-        to = out.at[pl.ds(pl.multiple_of(sc[S_K + j] * 128, 128), 128)]
+        to = out.at[pl.ds(pl.multiple_of(sc[S_K + first + j] * 128, 128), 128)]
         copies.append(pltpu.make_async_copy(wide.at[j], to, sems.at[j]))
         copies[-1].start()
     for copy in copies:
@@ -273,20 +313,32 @@
     table = call(stats_kernel, (sc, *lses), sds((NP, NP, 128), F32), scratch=[VMEM((NP, 128), F32)])
     lse_all = lax.all_to_all(table, INNER, 0, 0, tiled=True)
 
-    block = call(
-        moment_kernel, (sc, lse_all, *probs, *peaks, *chunks),
-        sds((8, ROWS_OUT, 1024), BF16),
-        in_specs=[INSIDE] * (1 + 2 * len(CHUNKS)) + [ANY] * len(CHUNKS),
-        scratch=[
-            VMEM((128 * NP, 1024), BF16), VMEM((1024, 128 * NP), BF16), VMEM((NP, 128), F32),
-            pltpu.SemaphoreType.DMA((len(CHUNKS),)),
-        ],
-        limit=24, flops=2 * 1024 * 2048 * 1024, moved_bytes=10_000_000,
-    )
-    mine = lax.all_to_all(block, GRP, 0, 0, tiled=True)
+    many = len(CHUNKS)
+    far_b, resp1, rows, total = call(
+        moment_far_kernel, (sc, lse_all, *probs, *peaks, *chunks),
+        [sds((512, 512), BF16), sds((512, 128 * NP), BF16), sds((128 * NP, 1024), BF16), sds((NP, 128), F32)],
+        in_specs=[INSIDE] * (1 + 2 * many) + [ANY] * many,
+        scratch=[pltpu.SemaphoreType.DMA((many,))],
+        limit=24, flops=2 * 512 * 2048 * 512, moved_bytes=8_000_000,
+    )
+    got_far_b = sent(far_b, "yl", 1)
+    *own_a, resp0 = call(
+        moment_a_kernel, (sc, total, resp1, rows, *probs, *peaks),
+        [sds((2, 136, 512), F32)] + [sds((2, 136, 512), BF16)] * 3 + [sds((512, 128 * NP), BF16)],
+        limit=24, flops=4 * 512 * 2048 * 512, moved_bytes=8_000_000,
+    )
+    got_a = [sent(own_a[d], "x", d) for d in (2, 1, 3)]
+    own_b = call(
+        moment_b_kernel, (sc, resp0, rows, got_far_b),
+        [sds((128, 512), F32)] + [sds((128, 512), BF16)] * 3,
+        limit=24, flops=2 * 512 * 2048 * 512, moved_bytes=6_000_000,
+    )
+    got_b = [sent(own_b[d], "x", d) for d in (2, 1, 3)]
+    keep_a, send_a = call(sum_a_kernel, (sc, own_a[0], *got_a), [sds((136, 512), F32), sds((136, 512), BF16)])
+    got_last_a = sent(send_a, "yl", 1)
 
     low, keep, send = call(
-        update_kernel, (sc, mine, prior, coarse, coarse_sq),
+        update_kernel, (sc, keep_a, got_last_a, own_b[0], *got_b, prior, coarse, coarse_sq),
         [sds((128, 1024), BF16), sds((64, 40, 128), F32), sds((64, 40, 128), BF16)],
         scratch=[VMEM((512, 128), BF16)], flops=300_000_000, moved_bytes=6_000_000,
     )
@@ -300,14 +352,24 @@
     new = call(coarse_kernel, (sc, parts, coarse), sds((64, 32, 128), BF16))
     mine_new = lax.all_to_all(new, CHIPS, 0, 0, tiled=True)
     other_new = moved(mine_new, ("c",), (1,))
+    out_scratch = [VMEM((4, 128, 1024), F32), pltpu.SemaphoreType.DMA((4,))]
+    fine_half = call(
+        functools.partial(fine_out_kernel, 0), (sc, *lows[:4]), sds((1024, 1024), F32),
+        out_specs=ANY, scratch=out_scratch, limit=8, moved_bytes=3_000_000,
+    )
     fine_update = call(
-        fine_out_kernel, (sc, *lows), sds((1024, 1024), F32), out_specs=ANY,
-        scratch=[VMEM((8, 128, 1024), F32), pltpu.SemaphoreType.DMA((8,))], limit=8,
-        flops=1_000_000, moved_bytes=6_000_000,
+        functools.partial(fine_out_kernel, 4), (sc, *lows[4:], fine_half), sds((1024, 1024), F32),
+        in_specs=[INSIDE] * 4 + [ANY], out_specs=ANY, scratch=out_scratch, limit=8, aliases={5: 0},
+        moved_bytes=3_000_000,
+    )
+    half_scratch = [VMEM((256, 1024), F32), pltpu.SemaphoreType.DMA]
+    coarse_half = call(
+        functools.partial(coarse_out_kernel, 0), (sc, mine_new), sds((512, 1024), F32),
+        out_specs=ANY, scratch=half_scratch, limit=8, moved_bytes=2_000_000,
     )
     coarse_update = call(
-        coarse_out_kernel, (sc, mine_new, other_new), sds((512, 1024), F32), out_specs=ANY,
-        scratch=[VMEM((512, 1024), F32), pltpu.SemaphoreType.DMA((2,))], limit=8,
+        functools.partial(coarse_out_kernel, 1), (sc, other_new, coarse_half), sds((512, 1024), F32),
+        in_specs=[INSIDE, ANY], out_specs=ANY, scratch=half_scratch, limit=8, aliases={2: 0}, moved_bytes=2_000_000,
     )
     return fine_update, coarse_update
 

time: 165 us -> 164 us (level)
  blocking collectives: 61.1 us -> 30.5 us
  waiting for transfers between devices: 27.4 us -> 41.6 us
  starting transfers between devices: 43.4 us -> 53.7 us
  Pallas kernels: 27.9 us -> 32.8 us
    all_to_all x1 -> x0, blocking collectives: 31.7 us -> none  [step(): mine = lax.all_to_all(block, GRP, 0, 0, tiled=True)]
    ppermute x24 -> x32, waiting for transfers between devices: 21.7 us -> 35.8 us  [moved(): return lax.ppermute(x, axes, perm)]
    ppermute x24 -> x32, starting transfers between devices: 37.9 us -> 48.2 us  [moved(): return lax.ppermute(x, axes, perm)]
    pallas_call x12 -> x17, Pallas kernels: 27.9 us -> 32.8 us  [call(): pl.pallas_call(kernel, in_specs=[SMEM, *(in_specs or [INSIDE] * (len(ins)...]
  transfers between devices with their start and end apart: 25 -> 33, of which waited for: 9 -> 13; matrix products, arithmetic and copies ran while one was open for 0% -> 0% of each run, Pallas kernels for 8% -> 13%
where the time goes in v1:
time: 164 us; the launch traced here: 163 us
  starting transfers between devices  53.7 us (33%)
  waiting for transfers between devices  41.6 us (25%)
  Pallas kernels  32.8 us (20%)
  blocking collectives  30.5 us (19%)
  local copies, waits for them, and re-layouts  2.82 us (2%)
    ppermute x32, starting transfers between devices, moved(): return lax.ppermute(x, axes, perm)  48.2 us
    ppermute x32, waiting for transfers between devices, moved(): return lax.ppermute(x, axes, perm)  35.8 us
    pallas_call x17, Pallas kernels, call(): pl.pallas_call(kernel, in_specs=[SMEM, *(in_specs or [INSIDE] * (len(ins)...  32.8 us
    all_to_all x1, blocking collectives, step(): parts = lax.all_to_all(half, CHIPS, 0, 0, tiled=True)  18.4 us
    all_to_all x1, blocking collectives, step(): lse_all = lax.all_to_all(table, INNER, 0, 0, tiled=True)  12.1 us
    all_to_all x1, waiting for transfers between devices, step(): mine_new = lax.all_to_all(new, CHIPS, 0, 0, tiled=True)  5.75 us
    all_to_all x1, starting transfers between devices, step(): mine_new = lax.all_to_all(new, CHIPS, 0, 0, tiled=True)  5.54 us
  transfers between devices with their start and end apart: 33, of which 13 were waited for; matrix products, arithmetic and copies ran while one was open for 0% of the time, Pallas kernels for 13%

profile of v1, /device:TPU:1, one launch (start us, length us, event | category | flops | bytes accessed | tf_op | source)
XLA Modules:
  0.0 163.3 jit_solution(3767438970816247467)
XLA Ops:
  0.6 3.8 %collective-permute-start.1 = (bf16[128,1024]{1,0:T(8,128)(2,1)}, bf16[128,1024]{1,0:T(8,128)(2,1)S(1)}, u32[]{:S(2)}, u32[]{:S(2)}) collective-permute-start(bf16[128,1024]{1,0:T(8,128)(2,1)} %refs_0_.1), channel_id=1, source_target_pairs={{0,8},{8,0},{1,9},{9,1},{2,10},{10,2},{3,11},{11,3},{4,12},{12,4},... | collective-permute-start | bytes 786440 | tf_op jit(solution)/shard_map/ppermute | solution.py:44
  5.4 3.8 %collective-permute-start.5 = (bf16[128,1024]{1,0:T(8,128)(2,1)}, bf16[128,1024]{1,0:T(8,128)(2,1)S(1)}, u32[]{:S(2)}, u32[]{:S(2)}) collective-permute-start(bf16[128,1024]{1,0:T(8,128)(2,1)} %refs_0_.1), channel_id=1, source_target_pairs={{0,6},{2,0},{4,2},{6,4},{1,7},{3,1},{5,3},{7,5},{8,14},{10,8},{12,... | collective-permute-start | bytes 786440 | tf_op jit(solution)/shard_map/ppermute | solution.py:44
  10.4 3.7 %collective-permute-start.9 = (bf16[128,1024]{1,0:T(8,128)(2,1)S(1)}, bf16[128,1024]{1,0:T(8,128)(2,1)S(1)}, u32[]{:S(2)}, u32[]{:S(2)}) collective-permute-start(bf16[128,1024]{1,0:T(8,128)(2,1)S(1)} %collective-permute-done.1.refs_0_), channel_id=1, source_target_pairs={{0,6},{2,0},{4,2},{6,4},{1,7},{3,1},{5,3},{7,5},{8,14},{10,8},{12,... | collective-permute-start | bytes 786440 | tf_op jit(solution)/shard_map/ppermute | solution.py:44
  19.9 3.4 %collective-permute-start.13 = (bf16[128,1024]{1,0:T(8,128)(2,1)S(1)}, bf16[128,1024]{1,0:T(8,128)(2,1)S(1)}, u32[]{:S(2)}, u32[]{:S(2)}) collective-permute-start(bf16[128,1024]{1,0:T(8,128)(2,1)S(1)} %collective-permute-done.9.refs_2_), channel_id=1, source_target_pairs={{0,6},{2,0},{4,2},{6,4},{1,7},{3,1},{5,3},{7,5},{8,14},{10,8},{12,... | collective-permute-start | bytes 786440 | tf_op jit(solution)/shard_map/ppermute | solution.py:44
  24.0 2.3 %collective-permute-start.4 = (bf16[128,1024]{1,0:T(8,128)(2,1)S(1)}, bf16[128,1024]{1,0:T(8,128)(2,1)S(1)}, u32[]{:S(2)}, u32[]{:S(2)}) collective-permute-start(bf16[128,1024]{1,0:T(8,128)(2,1)S(1)} %collective-permute-done.3.refs_0_), channel_id=1, source_target_pairs={{0,1},{1,0},{2,3},{3,2},{4,5},{5,4},{6,7},{7,6},{8,9},{9,8},{10,11... | collective-permute-start | bytes 786440 | tf_op jit(solution)/shard_map/ppermute | solution.py:44
  35.6 2.4 %shard_map.80 = (bf16[1024,512]{1,0:T(8,128)(2,1)S(1)}, f32[1,512]{1,0:T(1,128)S(1)}, f32[1,512]{1,0:T(1,128)S(1)}, bf16[512,1024]{1,0:T(8,128)(2,1)S(1)}) custom-call(s32[32]{0:T(128)S(1)} %pad_add_fusion.sc, bf16[1024,1024]{1,0:T(8,128)(2,1)S(1)} %copy-done, f32[1024,1]{1,0:T(8,128)S(1)} %get-tuple-element.43.fine_sq, ...), custom_call_target="tpu_custom_call" | custom-call | flops 1073741824 | bytes 4097152 | tf_op jit(solution)/shard_map/pallas_call | solution.py:54
  38.0 2.4 %shard_map.81 = (bf16[1024,512]{1,0:T(8,128)(2,1)S(1)}, f32[1,512]{1,0:T(1,128)S(1)}, f32[1,512]{1,0:T(1,128)S(1)}, bf16[512,1024]{1,0:T(8,128)(2,1)S(1)}) custom-call(s32[32]{0:T(128)S(1)} %pad_add_fusion.sc, bf16[1024,1024]{1,0:T(8,128)(2,1)S(1)} %copy-done, f32[1024,1]{1,0:T(8,128)S(1)} %get-tuple-element.43.fine_sq, ...), custom_call_target="tpu_custom_call" | custom-call | flops 1073741824 | bytes 4097152 | tf_op jit(solution)/shard_map/pallas_call | solution.py:54
  40.4 2.4 %shard_map.82 = (bf16[1024,512]{1,0:T(8,128)(2,1)S(1)}, f32[1,512]{1,0:T(1,128)S(1)}, f32[1,512]{1,0:T(1,128)S(1)}, bf16[512,1024]{1,0:T(8,128)(2,1)S(1)}) custom-call(s32[32]{0:T(128)S(1)} %pad_add_fusion.sc, bf16[1024,1024]{1,0:T(8,128)(2,1)S(1)} %copy-done, f32[1024,1]{1,0:T(8,128)S(1)} %get-tuple-element.43.fine_sq, ...), custom_call_target="tpu_custom_call" | custom-call | flops 1073741824 | bytes 4097152 | tf_op jit(solution)/shard_map/pallas_call | solution.py:54
  43.3 12.1 %all_to_all.15.lse_all = f32[16,16,128]{2,1,0:T(8,128)S(1)} all-to-all(f32[16,16,128]{2,1,0:T(8,128)S(1)} %shard_map.83), channel_id=1, replica_groups=mesh['yl'=2,'x'=4,'yh'=2,'z'=4,'c'=2] {'yh','z','c'}, dimensions={0} | all-to-all | bytes 262144 | tf_op jit(solution)/shard_map/all_to_all | solution.py:314
  55.5 2.9 %shard_map.84 = (bf16[512,512]{1,0:T(8,128)(2,1)S(1)}, bf16[512,2048]{1,0:T(8,128)(2,1)S(1)}, bf16[2048,1024]{1,0:T(8,128)(2,1)S(1)}, f32[16,128]{1,0:T(8,128)S(1)}) custom-call(s32[32]{0:T(128)S(1)} %pad_add_fusion.sc, f32[16,16,128]{2,1,0:T(8,128)S(1)} %all_to_all.15.lse_all, bf16[1024,256]{1,0:T(8,128)(2,1)S(1)} %get-tuple-element.49.refs_0_, ...), custom_call_target="tpu_custom_call" | custom-call | flops 1073741824 | bytes 8000000 | tf_op jit(solution)/shard_map/pallas_call | solution.py:54
  58.8 4.0 %shard_map.85 = (f32[2,136,512]{2,1,0:T(8,128)S(1)}, bf16[2,136,512]{2,1,0:T(8,128)(2,1)S(1)}, bf16[2,136,512]{2,1,0:T(8,128)(2,1)S(1)}, bf16[2,136,512]{2,1,0:T(8,128)(2,1)S(1)}, bf16[512,2048]{1,0:T(8,128)(2,1)S(1)}) custom-call(s32[32]{0:T(128)S(1)} %pad_add_fusion.sc, f32[16,128]{1,0:T(8,128)S(1)} %get-tuple-element.64.total, ...), custom_call_target="tpu_custom_call" | custom-call | flops 2147483648 | bytes 8000000 | tf_op jit(solution)/shard_map/pallas_call | solution.py:54
  62.8 2.8 %collective-permute-start.15 = (bf16[2,136,512]{2,1,0:T(8,128)(2,1)S(1)}, bf16[2,136,512]{2,1,0:T(8,128)(2,1)S(1)}, u32[]{:S(2)}, u32[]{:S(2)}) collective-permute-start(bf16[2,136,512]{2,1,0:T(8,128)(2,1)S(1)} %get-tuple-element.68), channel_id=1, source_target_pairs={{0,32},{16,48},{32,0},{48,16},{1,33},{17,49},{33,1},{49,17},{2,34}... | collective-permute-start | bytes 835592 | tf_op jit(solution)/shard_map/ppermute | solution.py:44
  66.0 2.3 %collective-permute-start.17 = (bf16[2,136,512]{2,1,0:T(8,128)(2,1)S(1)}, bf16[2,136,512]{2,1,0:T(8,128)(2,1)S(1)}, u32[]{:S(2)}, u32[]{:S(2)}) collective-permute-start(bf16[2,136,512]{2,1,0:T(8,128)(2,1)S(1)} %get-tuple-element.70), channel_id=1, source_target_pairs={{0,48},{16,0},{32,16},{48,32},{1,49},{17,1},{33,17},{49,33},{2,50}... | collective-permute-start | bytes 835592 | tf_op jit(solution)/shard_map/ppermute | solution.py:44
  68.3 3.4 %collective-permute-done.15.got1 = bf16[2,136,512]{2,1,0:T(8,128)(2,1)S(1)} collective-permute-done((bf16[2,136,512]{2,1,0:T(8,128)(2,1)S(1)}, bf16[2,136,512]{2,1,0:T(8,128)(2,1)S(1)}, u32[]{:S(2)}, u32[]{:S(2)}) %collective-permute-start.15) | collective-permute-done | bytes 278560 | tf_op jit(solution)/shard_map/ppermute | solution.py:44
  71.7 7.2 %collective-permute-done.16.got2 = bf16[2,136,512]{2,1,0:T(8,128)(2,1)S(1)} collective-permute-done((bf16[2,136,512]{2,1,0:T(8,128)(2,1)S(1)}, bf16[2,136,512]{2,1,0:T(8,128)(2,1)S(1)}, u32[]{:S(2)}, u32[]{:S(2)}) %collective-permute-start.16) | collective-permute-done | bytes 278560 | tf_op jit(solution)/shard_map/ppermute | solution.py:44
  88.5 3.6 %collective-permute-done.21.refs_4_ = bf16[128,512]{1,0:T(8,128)(2,1)S(1)} collective-permute-done((bf16[128,512]{1,0:T(8,128)(2,1)S(1)}, bf16[128,512]{1,0:T(8,128)(2,1)S(1)}, u32[]{:S(2)}, u32[]{:S(2)}) %collective-permute-start.21) | collective-permute-done | bytes 131104 | tf_op jit(solution)/shard_map/ppermute | solution.py:44
  97.3 18.4 %all_to_all.16.parts = bf16[64,40,128]{2,1,0:T(8,128)(2,1)S(1)} all-to-all(bf16[64,40,128]{2,1,0:T(8,128)(2,1)S(1)} %add_convert_fusion), channel_id=1, replica_groups=mesh['yl'=2,'x'=4,'yh'=2,'z'=4,'c'=2] {'yl','x','yh','z'}, dimensions={0} | all-to-all | bytes 1310720 | tf_op jit(solution)/shard_map/all_to_all | solution.py:351
  117.2 5.5 %all-to-all-start.2 = ((bf16[64,32,128]{2,1,0:T(8,128)(2,1)}), bf16[64,32,128]{2,1,0:T(8,128)(2,1)S(1)}, u32[]{:S(2)}, u32[]{:S(2)}) async-start(bf16[64,32,128]{2,1,0:T(8,128)(2,1)} %shard_map.91), calls=%async_computation.2 | async-start | bytes 1048576 | tf_op jit(solution)/shard_map/all_to_all | solution.py:353
  125.2 2.5 %collective-permute-start.28 = (bf16[128,1024]{1,0:T(8,128)(2,1)S(1)}, bf16[128,1024]{1,0:T(8,128)(2,1)S(1)}, u32[]{:S(2)}, u32[]{:S(2)}) collective-permute-start(bf16[128,1024]{1,0:T(8,128)(2,1)S(1)} %get-tuple-element.81.refs_0_), channel_id=1, source_target_pairs={{0,32},{16,48},{32,0},{48,16},{1,33},{17,49},{33,1},{49,17},{2,34}... | collective-permute-start | bytes 786440 | tf_op jit(solution)/shard_map/ppermute | solution.py:44
  127.7 5.7 %all-to-all-done.2.src = bf16[64,32,128]{2,1,0:T(8,128)(2,1)S(1)} async-done(((bf16[64,32,128]{2,1,0:T(8,128)(2,1)}), bf16[64,32,128]{2,1,0:T(8,128)(2,1)S(1)}, u32[]{:S(2)}, u32[]{:S(2)}) %all-to-all-start.2) | async-done | bytes 524320 | tf_op jit(solution)/shard_map/all_to_all | solution.py:353
  133.4 5.4 %collective-permute-start.31 = (bf16[64,32,128]{2,1,0:T(8,128)(2,1)S(1)}, bf16[64,32,128]{2,1,0:T(8,128)(2,1)S(1)}, u32[]{:S(2)}, u32[]{:S(2)}) collective-permute-start(bf16[64,32,128]{2,1,0:T(8,128)(2,1)S(1)} %all-to-all-done.2.src), channel_id=1, source_target_pairs={{0,1},{1,0},{2,3},{3,2},{4,5},{5,4},{6,7},{7,6},{8,9},{9,8},{10,11... | collective-permute-start | bytes 1572872 | tf_op jit(solution)/shard_map/ppermute | solution.py:44
  142.8 3.9 %collective-permute-done.27.refs_1_ = bf16[128,1024]{1,0:T(8,128)(2,1)S(1)} collective-permute-done((bf16[128,1024]{1,0:T(8,128)(2,1)S(1)}, bf16[128,1024]{1,0:T(8,128)(2,1)S(1)}, u32[]{:S(2)}, u32[]{:S(2)}) %collective-permute-start.27) | collective-permute-done | bytes 262176 | tf_op jit(solution)/shard_map/ppermute | solution.py:44
  149.1 4.8 %collective-permute-done.25.refs_2_ = bf16[128,1024]{1,0:T(8,128)(2,1)S(1)} collective-permute-done((bf16[128,1024]{1,0:T(8,128)(2,1)S(1)}, bf16[128,1024]{1,0:T(8,128)(2,1)S(1)}, u32[]{:S(2)}, u32[]{:S(2)}) %collective-permute-start.25) | collective-permute-done | bytes 262176 | tf_op jit(solution)/shard_map/ppermute | solution.py:44
  153.9 4.1 %collective-permute-done.24.refs_1_ = bf16[128,1024]{1,0:T(8,128)(2,1)S(1)} collective-permute-done((bf16[128,1024]{1,0:T(8,128)(2,1)S(1)}, bf16[128,1024]{1,0:T(8,128)(2,1)S(1)}, u32[]{:S(2)}, u32[]{:S(2)}) %collective-permute-start.24) | collective-permute-done | bytes 262176 | tf_op jit(solution)/shard_map/ppermute | solution.py:44
  (73 shorter events, 49.4 us)
Async XLA Ops:
  0.6 9.8 %collective-permute-start.1 = (bf16[128,1024]{1,0:T(8,128)(2,1)}, bf16[128,1024]{1,0:T(8,128)(2,1)S(1)}, u32[]{:S(2)}, u32[]{:S(2)}) collective-permute-start(bf16[128,1024]{1,0:T(8,128)(2,1)} %refs_0_.1), channel_id=1, source_target_pairs={{0,8},{8,0},{1,9},{9,1},{2,10},{10,2},{3,11},{11,3},{4,12},{12,4},... | collective-permute-start | bytes 786440 | tf_op jit(solution)/shard_map/ppermute | solution.py:44
  4.4 9.8 %collective-permute-start = (bf16[128,1024]{1,0:T(8,128)(2,1)}, bf16[128,1024]{1,0:T(8,128)(2,1)S(1)}, u32[]{:S(2)}, u32[]{:S(2)}) collective-permute-start(bf16[128,1024]{1,0:T(8,128)(2,1)} %refs_0_.1), channel_id=1, source_target_pairs={{0,1},{1,0},{2,3},{3,2},{4,5},{5,4},{6,7},{7,6},{8,9},{9,8},{10,11... | collective-permute-start | bytes 786440 | tf_op jit(solution)/shard_map/ppermute | solution.py:44
  5.4 10.6 %collective-permute-start.5 = (bf16[128,1024]{1,0:T(8,128)(2,1)}, bf16[128,1024]{1,0:T(8,128)(2,1)S(1)}, u32[]{:S(2)}, u32[]{:S(2)}) collective-permute-start(bf16[128,1024]{1,0:T(8,128)(2,1)} %refs_0_.1), channel_id=1, source_target_pairs={{0,6},{2,0},{4,2},{6,4},{1,7},{3,1},{5,3},{7,5},{8,14},{10,8},{12,... | collective-permute-start | bytes 786440 | tf_op jit(solution)/shard_map/ppermute | solution.py:44
  9.2 9.0 %collective-permute-start.3 = (bf16[128,1024]{1,0:T(8,128)(2,1)}, bf16[128,1024]{1,0:T(8,128)(2,1)S(1)}, u32[]{:S(2)}, u32[]{:S(2)}) collective-permute-start(bf16[128,1024]{1,0:T(8,128)(2,1)} %refs_0_.1), channel_id=1, source_target_pairs={{0,2},{2,4},{4,6},{6,0},{1,3},{3,5},{5,7},{7,1},{8,10},{10,12},{12... | collective-permute-start | bytes 786440 | tf_op jit(solution)/shard_map/ppermute | solution.py:44
  10.4 9.5 %collective-permute-start.9 = (bf16[128,1024]{1,0:T(8,128)(2,1)S(1)}, bf16[128,1024]{1,0:T(8,128)(2,1)S(1)}, u32[]{:S(2)}, u32[]{:S(2)}) collective-permute-start(bf16[128,1024]{1,0:T(8,128)(2,1)S(1)} %collective-permute-done.1.refs_0_), channel_id=1, source_target_pairs={{0,6},{2,0},{4,2},{6,4},{1,7},{3,1},{5,3},{7,5},{8,14},{10,8},{12,... | collective-permute-start | bytes 786440 | tf_op jit(solution)/shard_map/ppermute | solution.py:44
  14.2 9.8 %collective-permute-start.7 = (bf16[128,1024]{1,0:T(8,128)(2,1)S(1)}, bf16[128,1024]{1,0:T(8,128)(2,1)S(1)}, u32[]{:S(2)}, u32[]{:S(2)}) collective-permute-start(bf16[128,1024]{1,0:T(8,128)(2,1)S(1)} %collective-permute-done.1.refs_0_), channel_id=1, source_target_pairs={{0,2},{2,4},{4,6},{6,0},{1,3},{3,5},{5,7},{7,1},{8,10},{10,12},{12... | collective-permute-start | bytes 786440 | tf_op jit(solution)/shard_map/ppermute | solution.py:44
  14.2 12.2 %collective-permute-start.2 = (bf16[128,1024]{1,0:T(8,128)(2,1)S(1)}, bf16[128,1024]{1,0:T(8,128)(2,1)S(1)}, u32[]{:S(2)}, u32[]{:S(2)}) collective-permute-start(bf16[128,1024]{1,0:T(8,128)(2,1)S(1)} %collective-permute-done.1.refs_0_), channel_id=1, source_target_pairs={{0,1},{1,0},{2,3},{3,2},{4,5},{5,4},{6,7},{7,6},{8,9},{9,8},{10,11... | collective-permute-start | bytes 786440 | tf_op jit(solution)/shard_map/ppermute | solution.py:44
  16.0 10.5 %collective-permute-start.6 = (bf16[128,1024]{1,0:T(8,128)(2,1)S(1)}, bf16[128,1024]{1,0:T(8,128)(2,1)S(1)}, u32[]{:S(2)}, u32[]{:S(2)}) collective-permute-start(bf16[128,1024]{1,0:T(8,128)(2,1)S(1)} %collective-permute-done.5.refs_2_), channel_id=1, source_target_pairs={{0,1},{1,0},{2,3},{3,2},{4,5},{5,4},{6,7},{7,6},{8,9},{9,8},{10,11... | collective-permute-start | bytes 786440 | tf_op jit(solution)/shard_map/ppermute | solution.py:44
  18.2 13.7 %collective-permute-start.11 = (bf16[128,1024]{1,0:T(8,128)(2,1)S(1)}, bf16[128,1024]{1,0:T(8,128)(2,1)S(1)}, u32[]{:S(2)}, u32[]{:S(2)}) collective-permute-start(bf16[128,1024]{1,0:T(8,128)(2,1)S(1)} %collective-permute-done.3.refs_0_), channel_id=1, source_target_pairs={{0,2},{2,4},{4,6},{6,0},{1,3},{3,5},{5,7},{7,1},{8,10},{10,12},{12... | collective-permute-start | bytes 786440 | tf_op jit(solution)/shard_map/ppermute | solution.py:44
  19.9 12.1 %collective-permute-start.13 = (bf16[128,1024]{1,0:T(8,128)(2,1)S(1)}, bf16[128,1024]{1,0:T(8,128)(2,1)S(1)}, u32[]{:S(2)}, u32[]{:S(2)}) collective-permute-start(bf16[128,1024]{1,0:T(8,128)(2,1)S(1)} %collective-permute-done.9.refs_2_), channel_id=1, source_target_pairs={{0,6},{2,0},{4,2},{6,4},{1,7},{3,1},{5,3},{7,5},{8,14},{10,8},{12,... | collective-permute-start | bytes 786440 | tf_op jit(solution)/shard_map/ppermute | solution.py:44
  24.0 11.6 %collective-permute-start.4 = (bf16[128,1024]{1,0:T(8,128)(2,1)S(1)}, bf16[128,1024]{1,0:T(8,128)(2,1)S(1)}, u32[]{:S(2)}, u32[]{:S(2)}) collective-permute-start(bf16[128,1024]{1,0:T(8,128)(2,1)S(1)} %collective-permute-done.3.refs_0_), channel_id=1, source_target_pairs={{0,1},{1,0},{2,3},{3,2},{4,5},{5,4},{6,7},{7,6},{8,9},{9,8},{10,11... | collective-permute-start | bytes 786440 | tf_op jit(solution)/shard_map/ppermute | solution.py:44
  26.4 11.6 %collective-permute-start.10 = (bf16[128,1024]{1,0:T(8,128)(2,1)S(1)}, bf16[128,1024]{1,0:T(8,128)(2,1)S(1)}, u32[]{:S(2)}, u32[]{:S(2)}) collective-permute-start(bf16[128,1024]{1,0:T(8,128)(2,1)S(1)} %collective-permute-done.9.refs_2_), channel_id=1, source_target_pairs={{0,1},{1,0},{2,3},{3,2},{4,5},{5,4},{6,7},{7,6},{8,9},{9,8},{10,11... | collective-permute-start | bytes 786440 | tf_op jit(solution)/shard_map/ppermute | solution.py:44
  26.5 11.5 %collective-permute-start.8 = (bf16[128,1024]{1,0:T(8,128)(2,1)S(1)}, bf16[128,1024]{1,0:T(8,128)(2,1)S(1)}, u32[]{:S(2)}, u32[]{:S(2)}) collective-permute-start(bf16[128,1024]{1,0:T(8,128)(2,1)S(1)} %collective-permute-done.7.refs_0_), channel_id=1, source_target_pairs={{0,1},{1,0},{2,3},{3,2},{4,5},{5,4},{6,7},{7,6},{8,9},{9,8},{10,11... | collective-permute-start | bytes 786440 | tf_op jit(solution)/shard_map/ppermute | solution.py:44
  58.3 22.7 %collective-permute-start.19 = (bf16[512,512]{1,0:T(8,128)(2,1)S(1)}, bf16[512,512]{1,0:T(8,128)(2,1)S(1)}, u32[]{:S(2)}, u32[]{:S(2)}) collective-permute-start(bf16[512,512]{1,0:T(8,128)(2,1)S(1)} %get-tuple-element.74), channel_id=1, source_target_pairs={{0,64},{64,0},{1,65},{65,1},{2,66},{66,2},{3,67},{67,3},{4,68},{68... | collective-permute-start | bytes 1572872 | tf_op jit(solution)/shard_map/ppermute | solution.py:44
  65.6 13.3 %collective-permute-start.16 = (bf16[2,136,512]{2,1,0:T(8,128)(2,1)S(1)}, bf16[2,136,512]{2,1,0:T(8,128)(2,1)S(1)}, u32[]{:S(2)}, u32[]{:S(2)}) collective-permute-start(bf16[2,136,512]{2,1,0:T(8,128)(2,1)S(1)} %get-tuple-element.69), channel_id=1, source_target_pairs={{0,16},{16,32},{32,48},{48,0},{1,17},{17,33},{33,49},{49,1},{2,18}... | collective-permute-start | bytes 835592 | tf_op jit(solution)/shard_map/ppermute | solution.py:44
  66.0 13.0 %collective-permute-start.17 = (bf16[2,136,512]{2,1,0:T(8,128)(2,1)S(1)}, bf16[2,136,512]{2,1,0:T(8,128)(2,1)S(1)}, u32[]{:S(2)}, u32[]{:S(2)}) collective-permute-start(bf16[2,136,512]{2,1,0:T(8,128)(2,1)S(1)} %get-tuple-element.70), channel_id=1, source_target_pairs={{0,48},{16,0},{32,16},{48,32},{1,49},{17,1},{33,17},{49,33},{2,50}... | collective-permute-start | bytes 835592 | tf_op jit(solution)/shard_map/ppermute | solution.py:44
  117.2 16.2 %all-to-all-start.2 = ((bf16[64,32,128]{2,1,0:T(8,128)(2,1)}), bf16[64,32,128]{2,1,0:T(8,128)(2,1)S(1)}, u32[]{:S(2)}, u32[]{:S(2)}) async-start(bf16[64,32,128]{2,1,0:T(8,128)(2,1)} %shard_map.91), calls=%async_computation.2 | async-start | bytes 1048576 | tf_op jit(solution)/shard_map/all_to_all | solution.py:353
  122.8 16.3 %collective-permute-start.23 = (bf16[128,1024]{1,0:T(8,128)(2,1)S(1)}, bf16[128,1024]{1,0:T(8,128)(2,1)S(1)}, u32[]{:S(2)}, u32[]{:S(2)}) collective-permute-start(bf16[128,1024]{1,0:T(8,128)(2,1)S(1)} %get-tuple-element.81.refs_0_), channel_id=1, source_target_pairs={{0,64},{64,0},{1,65},{65,1},{2,66},{66,2},{3,67},{67,3},{4,68},{68... | collective-permute-start | bytes 786440 | tf_op jit(solution)/shard_map/ppermute | solution.py:44
  124.0 16.4 %collective-permute-start.29 = (bf16[128,1024]{1,0:T(8,128)(2,1)S(1)}, bf16[128,1024]{1,0:T(8,128)(2,1)S(1)}, u32[]{:S(2)}, u32[]{:S(2)}) collective-permute-start(bf16[128,1024]{1,0:T(8,128)(2,1)S(1)} %get-tuple-element.81.refs_0_), channel_id=1, source_target_pairs={{0,16},{16,32},{32,48},{48,0},{1,17},{17,33},{33,49},{49,1},{2,18}... | collective-permute-start | bytes 786440 | tf_op jit(solution)/shard_map/ppermute | solution.py:44
  125.2 16.2 %collective-permute-start.28 = (bf16[128,1024]{1,0:T(8,128)(2,1)S(1)}, bf16[128,1024]{1,0:T(8,128)(2,1)S(1)}, u32[]{:S(2)}, u32[]{:S(2)}) collective-permute-start(bf16[128,1024]{1,0:T(8,128)(2,1)S(1)} %get-tuple-element.81.refs_0_), channel_id=1, source_target_pairs={{0,32},{16,48},{32,0},{48,16},{1,33},{17,49},{33,1},{49,17},{2,34}... | collective-permute-start | bytes 786440 | tf_op jit(solution)/shard_map/ppermute | solution.py:44
  133.4 28.1 %collective-permute-start.31 = (bf16[64,32,128]{2,1,0:T(8,128)(2,1)S(1)}, bf16[64,32,128]{2,1,0:T(8,128)(2,1)S(1)}, u32[]{:S(2)}, u32[]{:S(2)}) collective-permute-start(bf16[64,32,128]{2,1,0:T(8,128)(2,1)S(1)} %all-to-all-done.2.src), channel_id=1, source_target_pairs={{0,1},{1,0},{2,3},{3,2},{4,5},{5,4},{6,7},{7,6},{8,9},{9,8},{10,11... | collective-permute-start | bytes 1572872 | tf_op jit(solution)/shard_map/ppermute | solution.py:44
  139.1 10.0 %collective-permute-start.26 = (bf16[128,1024]{1,0:T(8,128)(2,1)S(1)}, bf16[128,1024]{1,0:T(8,128)(2,1)S(1)}, u32[]{:S(2)}, u32[]{:S(2)}) collective-permute-start(bf16[128,1024]{1,0:T(8,128)(2,1)S(1)} %collective-permute-done.23.refs_0_), channel_id=1, source_target_pairs={{0,16},{16,32},{32,48},{48,0},{1,17},{17,33},{33,49},{49,1},{2,18}... | collective-permute-start | bytes 786440 | tf_op jit(solution)/shard_map/ppermute | solution.py:44
  140.3 13.6 %collective-permute-start.25 = (bf16[128,1024]{1,0:T(8,128)(2,1)S(1)}, bf16[128,1024]{1,0:T(8,128)(2,1)S(1)}, u32[]{:S(2)}, u32[]{:S(2)}) collective-permute-start(bf16[128,1024]{1,0:T(8,128)(2,1)S(1)} %collective-permute-done.23.refs_0_), channel_id=1, source_target_pairs={{0,32},{16,48},{32,0},{48,16},{1,33},{17,49},{33,1},{49,17},{2,34}... | collective-permute-start | bytes 786440 | tf_op jit(solution)/shard_map/ppermute | solution.py:44
  141.4 16.6 %collective-permute-start.24 = (bf16[128,1024]{1,0:T(8,128)(2,1)S(1)}, bf16[128,1024]{1,0:T(8,128)(2,1)S(1)}, u32[]{:S(2)}, u32[]{:S(2)}) collective-permute-start(bf16[128,1024]{1,0:T(8,128)(2,1)S(1)} %collective-permute-done.23.refs_0_), channel_id=1, source_target_pairs={{0,48},{16,0},{32,16},{48,32},{1,49},{17,1},{33,17},{49,33},{2,50}... | collective-permute-start | bytes 786440 | tf_op jit(solution)/shard_map/ppermute | solution.py:44
  (13 other events, 79.9 us)

commit v2 on v1

v2 whole, which is shorter than its diff:
```python
import functools

import numpy as np
import jax
import jax.numpy as jnp
from jax import lax
from jax.experimental import pallas as pl
from jax.experimental.pallas import tpu as pltpu
from jax.sharding import Mesh
from jax.sharding import PartitionSpec as P

GRP = ("yl", "x")
INNER = ("yh", "z", "c")
CHIPS = ("yl", "x", "yh", "z")
SIZES = {"yl": 2, "x": 4, "yh": 2, "z": 4, "c": 2}

F32 = jnp.float32
BF16 = jnp.bfloat16
shrink = 1.0
anchor = 8.0
inv_temper = 50.0
NT = (((1,), (1,)), ((), ()))
TN = (((0,), (0,)), ((), ()))
VMEM = pltpu.VMEM

CHUNKS = (
    ((0, 0, 0), (0, 0, 1), (1, 0, 0), (1, 0, 1)),
    ((0, 1, 0), (0, 1, 1), (0, 3, 0), (0, 3, 1)),
    ((0, 2, 0), (0, 2, 1), (1, 2, 0), (1, 2, 1)),
    ((1, 1, 0), (1, 1, 1), (1, 3, 0), (1, 3, 1)),
)
PIECES = tuple(p for chunk in CHUNKS for p in chunk)
NP = len(PIECES)


def position():
    return tuple(lax.axis_index(a) for a in ("yl", "x", "yh", "z", "c"))


def fine_block(j):
    yl, x, _, _, _ = position()
    return (yl ^ (j // 4)) * 4 + (x + j % 4) % 4


def piece_owner(i):
    _, _, yh, z, c = position()
    dyh, dz, dc = PIECES[i]
    return ((yh ^ dyh) * 4 + (z + 4 - dz) % 4) * 2 + (c ^ dc)


def rows_at(block, size):
    return pl.ds(pl.multiple_of(block * size, size), size)


def moved(x, axes, shifts):
    sizes = [SIZES[a] for a in axes]
    perm = []
    for idx in np.ndindex(*sizes):
        to = [(i + s) % n for i, s, n in zip(idx, shifts, sizes)]
        perm.append((int(np.ravel_multi_index(idx, sizes)), int(np.ravel_multi_index(to, sizes))))
    return lax.ppermute(x, axes, perm)


INSIDE = pl.BlockSpec(memory_space=pltpu.VMEM)
ANY = pl.BlockSpec(memory_space=pl.ANY)
FAR = pl.BlockSpec(memory_space=pltpu.HBM)


def call(kernel, ins, outs, in_specs=None, out_specs=None, scratch=(), limit=16, aliases=None, flops=0, moved_bytes=0):
    many = isinstance(outs, (list, tuple))
    return pl.pallas_call(
        kernel,
        in_specs=in_specs or [INSIDE] * len(ins),
        out_specs=out_specs or ([INSIDE] * len(outs) if many else INSIDE),
        out_shape=outs,
        scratch_shapes=list(scratch),
        input_output_aliases=aliases or {},
        cost_estimate=pl.CostEstimate(flops=flops, bytes_accessed=moved_bytes, transcendentals=0),
        compiler_params=pltpu.CompilerParams(vmem_limit_bytes=limit * 1024 * 1024),
    )(*ins)


def sds(shape, dtype):
    return jax.ShapeDtypeStruct(shape, dtype)


def softmax_over_coarse(rows, coarse, coarse_sq):
    logits = (lax.dot_general(coarse, rows, NT, preferred_element_type=F32) - 0.5 * coarse_sq) * inv_temper
    shifted = jnp.exp(logits - jnp.max(logits, axis=0, keepdims=True))
    return shifted / jnp.sum(shifted, axis=0, keepdims=True)


def norms_kernel(fine_hbm, coarse_hbm, fine, coarse, fine_sq, coarse_sq, sems):
    copies = []
    for i in range(12):
        src, dst, at = (fine_hbm, fine, i) if i < 8 else (coarse_hbm, coarse, i - 8)
        rows = pl.ds(128 * at, 128)
        copies.append(pltpu.make_async_copy(src.at[rows], dst.at[rows], sems.at[i]))
        copies[-1].start()
    for i in range(12):
        src, dst, at = (fine, fine_sq, i) if i < 8 else (coarse, coarse_sq, i - 8)
        copies[i].wait()
        rows = slice(128 * at, 128 * at + 128)
        dst[rows, :] = jnp.sum(jnp.square(src[rows, :].astype(F32)), axis=1, keepdims=True)


def prior_kernel(fine, coarse, coarse_sq, prior):
    parent = softmax_over_coarse(fine[rows_at(fine_block(0), 128), :], coarse[...], coarse_sq[...]).astype(BF16)
    prior[...] = lax.dot_general(parent, coarse[...], TN, preferred_element_type=F32)


def scores_kernel(fine, fine_sq, *refs):
    n = len(refs) - 4
    pieces, (probs, peak, lse, rows) = refs[:n], refs[n:]
    for i in range(n):
        rows[128 * i : 128 * i + 128, :] = pieces[i][...]
    for b in range(n // 2):
        cols = slice(256 * b, 256 * b + 256)
        s = lax.dot_general(fine[...], rows[cols, :], NT, preferred_element_type=F32)
        s = (s - 0.5 * fine_sq[...]) * inv_temper
        top = jnp.max(s, axis=0, keepdims=True)
        p = jnp.exp(s - top)
        probs[:, cols] = p.astype(BF16)
        peak[:, cols] = top
        lse[:, cols] = top + jnp.log(jnp.sum(p, axis=0, keepdims=True))


def stats_kernel(*refs):
    lses, (out,), (table,) = refs[: len(CHUNKS)], refs[len(CHUNKS) : -1], refs[-1:]
    at = 0
    for chunk, lse in zip(CHUNKS, lses):
        for i in range(len(chunk)):
            table[pl.ds(piece_owner(at), 1), :] = lse[:, 128 * i : 128 * i + 128]
            at += 1
    for peer in range(NP):
        out[peer] = table[...]


def responsibilities(first, probs, peaks, total, resp):
    at = 0
    for chunk, prob, peak in zip(CHUNKS, probs, peaks):
        for i in range(len(chunk)):
            cols = slice(128 * i, 128 * i + 128)
            factor = jnp.exp(peak[:, cols] - total[pl.ds(piece_owner(at), 1), :])
            for j in range(4):
                part = prob[rows_at(fine_block(first + j), 128), cols].astype(F32) * factor
                resp[128 * j : 128 * j + 128, 128 * at : 128 * at + 128] = part.astype(BF16)
            at += 1


def product(resp, chunks, cols):
    total = None
    for i, chunk in enumerate(chunks):
        part = jnp.dot(resp[:, 512 * i : 512 * i + 512], chunk[:, cols], preferred_element_type=F32)
        total = part if total is None else total + part
    return total


def moment_far_kernel(lse_all, *refs):
    nc = len(CHUNKS)
    probs, peaks, chunks = refs[:nc], refs[nc : 2 * nc], refs[2 * nc : 3 * nc]
    out, resp, total = refs[3 * nc :]
    top = jnp.max(lse_all[...], axis=0)
    total[...] = top + jnp.log(jnp.sum(jnp.exp(lse_all[...] - top[None]), axis=0))
    responsibilities(4, probs, peaks, total, resp)
    for n in range(2):
        part = product(resp, chunks, slice(512 + 256 * n, 768 + 256 * n))
        out[:, 256 * n : 256 * n + 256] = part.astype(BF16)


def moment_a_kernel(total, resp1, *refs):
    nc = len(CHUNKS)
    probs, peaks, chunks = refs[:nc], refs[nc : 2 * nc], refs[2 * nc : 3 * nc]
    outs, resp0 = refs[3 * nc : 3 * nc + 4], refs[-1]
    responsibilities(0, probs, peaks, total, resp0)
    line = lax.broadcasted_iota(jnp.int32, (8, 128), 0)
    for h, resp in ((1, resp1), (0, resp0)):
        mass = lax.dot_general(jnp.ones((8, 128 * NP), BF16), resp[...], NT, preferred_element_type=F32)
        high = mass.astype(BF16).astype(F32)
        low = mass - high
        for n in range(2):
            cols = slice(256 * n, 256 * n + 256)
            part = product(resp, chunks, cols)
            for j in range(4):
                outs[j][h, 0:128, cols] = part[128 * j : 128 * j + 128].astype(outs[j].dtype)
        for j in range(4):
            cols = slice(128 * j, 128 * j + 128)
            both = jnp.where(line == 0, high[:, cols], jnp.where(line == 1, low[:, cols], 0.0))
            outs[j][h, 128:136, :] = jnp.zeros((8, 512), outs[j].dtype)
            outs[j][h, 128:136, 0:128] = both.astype(outs[j].dtype)


def moment_b_kernel(resp0, got, *refs):
    chunks, outs = refs[: len(CHUNKS)], refs[len(CHUNKS) :]
    for n in range(2):
        cols = slice(256 * n, 256 * n + 256)
        part = product(resp0, chunks, slice(512 + 256 * n, 768 + 256 * n)) + got[:, cols].astype(F32)
        for j in range(4):
            outs[j][:, cols] = part[128 * j : 128 * j + 128].astype(outs[j].dtype)


def sum_a_kernel(own, got1, got2, got3, keep, send):
    sums = [own[h] + got1[h].astype(F32) + got2[h].astype(F32) + got3[h].astype(F32) for h in range(2)]
    keep[...] = sums[0]
    mass = sums[1][128:129] + sums[1][129:130]
    high = mass.astype(BF16).astype(F32)
    line = lax.broadcasted_iota(jnp.int32, (8, 512), 0)
    both = jnp.where(line == 0, high, jnp.where(line == 1, mass - high, 0.0))
    send[0:128, :] = sums[1][0:128].astype(BF16)
    send[128:136, :] = both.astype(BF16)


def update_kernel(*refs):
    keep_a, got_a, own_b, got_b, (prior, coarse, coarse_sq, low_out, keep, send, shares) = (
        refs[0], refs[1], refs[2], refs[3:6], refs[6:],
    )
    left = prior[:, 0:512] + keep_a[0:128, :] + got_a[0:128, :].astype(F32)
    right = prior[:, 512:1024] + own_b[...]
    for got in got_b:
        right = right + got[...].astype(F32)
    moment = jnp.concatenate([left, right], axis=1)
    tail = keep_a[128:136, 0:128] + got_a[128:136, 0:128].astype(F32)
    mass = tail[0:1] + tail[1:2]
    weight = mass + shrink
    diag = lax.broadcasted_iota(jnp.int32, (128, 128), 0) == lax.broadcasted_iota(jnp.int32, (128, 128), 1)
    column = jnp.sum(jnp.where(diag, jnp.broadcast_to(weight, (128, 128)), 0.0), axis=1, keepdims=True)
    low = (moment / column).astype(BF16)
    low_out[...] = low
    child = softmax_over_coarse(low, coarse[...], coarse_sq[...])
    shares[...] = (child * weight).astype(BF16)
    den = lax.dot_general(jnp.ones((8, 128), BF16), shares[...], NT, preferred_element_type=F32)[0:1]
    high = den.astype(BF16).astype(F32)
    rest = den - high
    line = lax.broadcasted_iota(jnp.int32, (8, 128), 0)
    dens = jnp.zeros((8, 128), F32)
    for q in range(4):
        cols = slice(128 * q, 128 * q + 128)
        dens = jnp.where(line == q, jnp.broadcast_to(high[:, cols], (8, 128)), dens)
        dens = jnp.where(line == q + 4, jnp.broadcast_to(rest[:, cols], (8, 128)), dens)
    core = lax.axis_index("c")
    for out, half in ((keep, core), (send, 1 - core)):
        num = jnp.dot(shares[rows_at(half, 256), :], low, preferred_element_type=F32)
        for jr in range(8):
            for jc in range(8):
                out[jr * 8 + jc, 0:32, :] = num[32 * jr : 32 * jr + 32, 128 * jc : 128 * jc + 128].astype(out.dtype)
                out[jr * 8 + jc, 32:40, :] = dens.astype(out.dtype)


def coarse_kernel(parts, coarse, out):
    total = jnp.sum(parts[...].astype(F32), axis=0)
    yl, x, yh, z, c = position()
    mine = ((yl * 4 + x) * 2 + yh) * 4 + z
    at, col = c * 256 + (mine // 8) * 32, mine % 8
    dens = total[32:36] + total[36:40]
    line = lax.broadcasted_iota(jnp.int32, (4, 128), 0)
    row = jnp.sum(jnp.where(line == at // 128, dens, 0.0), axis=0, keepdims=True)
    r = lax.broadcasted_iota(jnp.int32, (32, 128), 0)
    lane = lax.broadcasted_iota(jnp.int32, (32, 128), 1)
    den = jnp.sum(jnp.where(lane == r + at % 128, jnp.broadcast_to(row, (32, 128)), 0.0), axis=1, keepdims=True)
    old = coarse[pl.ds(pl.multiple_of(at, 32), 32), pl.ds(pl.multiple_of(col * 128, 128), 128)]
    new = (total[0:32] + anchor * old.astype(F32)) / (den + anchor)
    out[...] = jnp.broadcast_to(new.astype(BF16)[None], (64, 32, 128))


def coarse_add_kernel(keep, got, out):
    out[...] = (keep[...] + got[...].astype(F32)).astype(BF16)


def coarse_out_kernel(mine, other, out, wide, sems):
    copies = []
    for i, (src, half) in enumerate(((mine, lax.axis_index("c")), (other, 1 - lax.axis_index("c")))):
        for q in range(2):
            for jr in range(4 * q, 4 * q + 4):
                for jc in range(8):
                    wide[i, 32 * jr : 32 * jr + 32, 128 * jc : 128 * jc + 128] = src[jr * 8 + jc].astype(F32)
            to = out.at[pl.ds(pl.multiple_of(half * 256 + 128 * q, 128), 128)]
            copies.append(pltpu.make_async_copy(wide.at[i, pl.ds(128 * q, 128)], to, sems.at[2 * i + q]))
            copies[-1].start()
    for copy in copies:
        copy.wait()


def fine_out_kernel(first, *refs):
    blocks, (out, wide, sems) = refs[:4], refs[-3:]
    copies = []
    for j in range(4):
        wide[j] = blocks[j][...].astype(F32)
        to = out.at[rows_at(fine_block(first + j), 128)]
        copies.append(pltpu.make_async_copy(wide.at[j], to, sems.at[j]))
        copies[-1].start()
    for copy in copies:
        copy.wait()


def step(embeds, fine, coarse):
    def sent(x, axis, by):
        return moved(x, (axis,), (by,))

    up = sent(embeds, "z", 1)
    down = sent(embeds, "z", 3)
    across = sent(embeds, "yh", 1)
    far = sent(embeds, "z", 2)
    corner = moved(embeds, ("yh", "z"), (1, 2))
    across_up = sent(across, "z", 1)
    across_down = sent(across, "z", 3)

    def with_twin(**blocks):
        both = []
        for x in blocks.values():
            both += [x, sent(x, "c", 1)]
        return both

    fine, coarse, fine_sq, coarse_sq = call(
        norms_kernel, (fine, coarse),
        [sds((1024, 1024), BF16), sds((512, 1024), BF16), sds((1024, 1), F32), sds((512, 1), F32)],
        in_specs=[FAR, FAR], scratch=[pltpu.SemaphoreType.DMA((12,))], limit=60, flops=3_000_000, moved_bytes=3_000_000,
    )

    inputs = (
        with_twin(own=embeds, across=across), with_twin(up=up, down=down),
        with_twin(far=far, corner=corner), with_twin(across_up=across_up, across_down=across_down),
    )
    probs, peaks, lses, chunks = [], [], [], []
    for blocks in inputs:
        width = 128 * len(blocks)
        prob, peak, lse, rows = call(
            scores_kernel, (fine, fine_sq, *blocks),
            [sds((1024, width), BF16), sds((1, width), F32), sds((1, width), F32), sds((width, 1024), BF16)],
            flops=2 * width * 1024 * 1024, moved_bytes=2_000_000 + width * 4096,
        )
        probs.append(prob)
        peaks.append(peak)
        lses.append(lse)
        chunks.append(rows)

    table = call(stats_kernel, lses, sds((NP, NP, 128), F32), scratch=[VMEM((NP, 128), F32)])
    lse_all = lax.all_to_all(table, INNER, 0, 0, tiled=True)

    far_b, resp1, total = call(
        moment_far_kernel, (lse_all, *probs, *peaks, *chunks),
        [sds((512, 512), BF16), sds((512, 128 * NP), BF16), sds((NP, 128), F32)],
        limit=24, flops=2 * 512 * 2048 * 512, moved_bytes=8_000_000,
    )
    got_far_b = sent(far_b, "yl", 1)
    *own_a, resp0 = call(
        moment_a_kernel, (total, resp1, *probs, *peaks, *chunks),
        [sds((2, 136, 512), F32)] + [sds((2, 136, 512), BF16)] * 3 + [sds((512, 128 * NP), BF16)],
        limit=24, flops=4 * 512 * 2048 * 512, moved_bytes=8_000_000,
    )
    prior = call(
        prior_kernel, (fine, coarse, coarse_sq), sds((128, 1024), F32),
        flops=300_000_000, moved_bytes=3_000_000,
    )
    got_a = [sent(own_a[d], "x", d) for d in (2, 1, 3)]
    own_b = call(
        moment_b_kernel, (resp0, got_far_b, *chunks),
        [sds((128, 512), F32)] + [sds((128, 512), BF16)] * 3,
        limit=24, flops=2 * 512 * 2048 * 512, moved_bytes=6_000_000,
    )
    got_b = [sent(own_b[d], "x", d) for d in (2, 1, 3)]
    keep_a, send_a = call(sum_a_kernel, (own_a[0], *got_a), [sds((136, 512), F32), sds((136, 512), BF16)])
    got_last_a = sent(send_a, "yl", 1)

    low, keep, send = call(
        update_kernel, (keep_a, got_last_a, own_b[0], *got_b, prior, coarse, coarse_sq),
        [sds((128, 1024), BF16), sds((64, 40, 128), F32), sds((64, 40, 128), BF16)],
        scratch=[VMEM((512, 128), BF16)], flops=300_000_000, moved_bytes=6_000_000,
    )
    twin = moved(send, ("c",), (1,))
    lows = [low] + [sent(low, "x", 4 - d) for d in (1, 2, 3)]
    partner = sent(low, "yl", 1)
    lows += [partner, sent(partner, "x", 3), sent(lows[2], "yl", 1), sent(partner, "x", 1)]

    half = call(coarse_add_kernel, (keep, twin), sds((64, 40, 128), BF16), moved_bytes=2_000_000)
    parts = lax.all_to_all(half, CHIPS, 0, 0, tiled=True)
    new = call(coarse_kernel, (parts, coarse), sds((64, 32, 128), BF16))
    mine_new = lax.all_to_all(new, CHIPS, 0, 0, tiled=True)
    other_new = moved(mine_new, ("c",), (1,))
    out_scratch = [VMEM((4, 128, 1024), F32), pltpu.SemaphoreType.DMA((4,))]
    fine_half = call(
        functools.partial(fine_out_kernel, 0), lows[:4], sds((1024, 1024), F32),
        out_specs=ANY, scratch=out_scratch, limit=8, moved_bytes=3_000_000,
    )
    fine_update = call(
        functools.partial(fine_out_kernel, 4), (*lows[4:], fine_half), sds((1024, 1024), F32),
        in_specs=[INSIDE] * 4 + [ANY], out_specs=ANY, scratch=out_scratch, limit=8, aliases={4: 0},
        moved_bytes=3_000_000,
    )
    coarse_update = call(
        coarse_out_kernel, (mine_new, other_new), sds((512, 1024), F32), out_specs=ANY,
        scratch=[VMEM((2, 256, 1024), F32), pltpu.SemaphoreType.DMA((4,))], limit=8, moved_bytes=3_000_000,
    )
    return fine_update, coarse_update


def solution(mesh):
    finer = Mesh(mesh.devices.reshape(2, 4, 2, 4, 2), ("yl", "x", "yh", "z", "c"))
    return jax.shard_map(
        step,
        mesh=finer,
        in_specs=(P((*GRP, *INNER), None), P(INNER, None), P()),
        out_specs=(P(INNER, None), P()),
        check_vma=False,
    )
```

time: 164 us -> 161 us (0.982)
  Pallas kernels: 32.8 us -> 25.9 us
  starting transfers between devices: 53.7 us -> 59.2 us
    pallas_call x17, Pallas kernels: 32.8 us -> 25.9 us  [call(): pl.pallas_call(kernel, in_specs=in_specs or [INSIDE] * len(ins), out_spec...]
    ppermute x32, starting transfers between devices: 48.2 us -> 53.6 us  [moved(): return lax.ppermute(x, axes, perm)]
    all_to_all x1, blocking collectives: 12.1 us -> 10.4 us  [step(): lse_all = lax.all_to_all(table, INNER, 0, 0, tiled=True)]
  transfers between devices with their start and end apart: 33 -> 33, of which waited for: 13 -> 12; matrix products, arithmetic and copies ran while one was open for 0% -> 0% of each run, Pallas kernels for 13% -> 12%
where the time goes in v2:
time: 161 us; the launch traced here: 160 us
  starting transfers between devices  59.2 us (37%)
  waiting for transfers between devices  42.4 us (26%)
  blocking collectives  29.1 us (18%)
  Pallas kernels  25.9 us (16%)
  local copies, waits for them, and re-layouts  2.65 us (2%)
    ppermute x32, starting transfers between devices, moved(): return lax.ppermute(x, axes, perm)  53.6 us
    ppermute x32, waiting for transfers between devices, moved(): return lax.ppermute(x, axes, perm)  36.3 us
    pallas_call x17, Pallas kernels, call(): pl.pallas_call(kernel, in_specs=in_specs or [INSIDE] * len(ins), out_spec...  25.9 us
    all_to_all x1, blocking collectives, step(): parts = lax.all_to_all(half, CHIPS, 0, 0, tiled=True)  18.8 us
    all_to_all x1, blocking collectives, step(): lse_all = lax.all_to_all(table, INNER, 0, 0, tiled=True)  10.4 us
    all_to_all x1, waiting for transfers between devices, step(): mine_new = lax.all_to_all(new, CHIPS, 0, 0, tiled=True)  6.1 us
    all_to_all x1, starting transfers between devices, step(): mine_new = lax.all_to_all(new, CHIPS, 0, 0, tiled=True)  5.54 us
  transfers between devices with their start and end apart: 33, of which 12 were waited for; matrix products, arithmetic and copies ran while one was open for 0% of the time, Pallas kernels for 12%

profile of v2, /device:TPU:1, one launch (start us, length us, event | category | flops | bytes accessed | tf_op | source)
XLA Modules:
  0.0 160.3 jit_solution(1498158496218675292)
XLA Ops:
  0.6 4.6 %collective-permute-start.5 = (bf16[128,1024]{1,0:T(8,128)(2,1)}, bf16[128,1024]{1,0:T(8,128)(2,1)S(1)}, u32[]{:S(2)}, u32[]{:S(2)}) collective-permute-start(bf16[128,1024]{1,0:T(8,128)(2,1)} %refs_0_.1), channel_id=1, source_target_pairs={{0,6},{2,0},{4,2},{6,4},{1,7},{3,1},{5,3},{7,5},{8,14},{10,8},{12,... | collective-permute-start | bytes 786440 | tf_op jit(solution)/shard_map/ppermute | solution.py:61
  5.3 2.9 %collective-permute-start.1 = (bf16[128,1024]{1,0:T(8,128)(2,1)}, bf16[128,1024]{1,0:T(8,128)(2,1)S(1)}, u32[]{:S(2)}, u32[]{:S(2)}) collective-permute-start(bf16[128,1024]{1,0:T(8,128)(2,1)} %refs_0_.1), channel_id=1, source_target_pairs={{0,8},{8,0},{1,9},{9,1},{2,10},{10,2},{3,11},{11,3},{4,12},{12,4},... | collective-permute-start | bytes 786440 | tf_op jit(solution)/shard_map/ppermute | solution.py:61
  15.7 7.5 %collective-permute-done.3.refs_0_ = bf16[128,1024]{1,0:T(8,128)(2,1)S(1)} collective-permute-done((bf16[128,1024]{1,0:T(8,128)(2,1)}, bf16[128,1024]{1,0:T(8,128)(2,1)S(1)}, u32[]{:S(2)}, u32[]{:S(2)}) %collective-permute-start.3) | collective-permute-done | bytes 262176 | tf_op jit(solution)/shard_map/ppermute | solution.py:61
  23.2 7.2 %collective-permute-start.10 = (bf16[128,1024]{1,0:T(8,128)(2,1)S(1)}, bf16[128,1024]{1,0:T(8,128)(2,1)S(1)}, u32[]{:S(2)}, u32[]{:S(2)}) collective-permute-start(bf16[128,1024]{1,0:T(8,128)(2,1)S(1)} %collective-permute-done.9.refs_2_), channel_id=1, source_target_pairs={{0,1},{1,0},{2,3},{3,2},{4,5},{5,4},{6,7},{7,6},{8,9},{9,8},{10,11... | collective-permute-start | bytes 786440 | tf_op jit(solution)/shard_map/ppermute | solution.py:61
  31.7 6.3 %collective-permute-start.2 = (bf16[128,1024]{1,0:T(8,128)(2,1)S(1)}, bf16[128,1024]{1,0:T(8,128)(2,1)S(1)}, u32[]{:S(2)}, u32[]{:S(2)}) collective-permute-start(bf16[128,1024]{1,0:T(8,128)(2,1)S(1)} %collective-permute-done.1.refs_2_), channel_id=1, source_target_pairs={{0,1},{1,0},{2,3},{3,2},{4,5},{5,4},{6,7},{7,6},{8,9},{9,8},{10,11... | collective-permute-start | bytes 786440 | tf_op jit(solution)/shard_map/ppermute | solution.py:61
  38.0 4.4 %shard_map.50 = (bf16[1024,1024]{1,0:T(8,128)(2,1)}, bf16[512,1024]{1,0:T(8,128)(2,1)}, f32[1024,1]{1,0:T(8,128)}, f32[512,1]{1,0:T(8,128)}) custom-call(bf16[1024,1024]{1,0:T(8,128)(2,1)} %fine_hbm.1, bf16[512,1024]{1,0:T(8,128)(2,1)} %coarse_hbm.1), custom_call_target="tpu_custom_call" | custom-call | flops 3000000 | bytes 3000000 | tf_op jit(solution)/shard_map/pallas_call | solution.py:71
  47.5 1.8 %shard_map.52 = (bf16[1024,512]{1,0:T(8,128)(2,1)S(1)}, f32[1,512]{1,0:T(1,128)S(1)}, f32[1,512]{1,0:T(1,128)S(1)}, bf16[512,1024]{1,0:T(8,128)(2,1)S(1)}) custom-call(bf16[1024,1024]{1,0:T(8,128)(2,1)S(1)} %copy-done.1, f32[1024,1]{1,0:T(8,128)S(1)} %copy-done.4, bf16[128,1024]{1,0:T(8,128)(2,1)S(1)} %collective-permute-done.3.refs_0_, ...), custom_call_target="tpu_custom_call" | custom-call | flops 1073741824 | bytes 4097152 | tf_op jit(solution)/shard_map/pallas_call | solution.py:71
  49.3 1.8 %shard_map.51 = (bf16[1024,512]{1,0:T(8,128)(2,1)S(1)}, f32[1,512]{1,0:T(1,128)S(1)}, f32[1,512]{1,0:T(1,128)S(1)}, bf16[512,1024]{1,0:T(8,128)(2,1)S(1)}) custom-call(bf16[1024,1024]{1,0:T(8,128)(2,1)S(1)} %copy-done.1, f32[1024,1]{1,0:T(8,128)S(1)} %copy-done.4, bf16[128,1024]{1,0:T(8,128)(2,1)S(1)} %copy-done.5, ...), custom_call_target="tpu_custom_call" | custom-call | flops 1073741824 | bytes 4097152 | tf_op jit(solution)/shard_map/pallas_call | solution.py:71
  51.1 1.8 %shard_map.54 = (bf16[1024,512]{1,0:T(8,128)(2,1)S(1)}, f32[1,512]{1,0:T(1,128)S(1)}, f32[1,512]{1,0:T(1,128)S(1)}, bf16[512,1024]{1,0:T(8,128)(2,1)S(1)}) custom-call(bf16[1024,1024]{1,0:T(8,128)(2,1)S(1)} %copy-done.1, f32[1024,1]{1,0:T(8,128)S(1)} %copy-done.4, bf16[128,1024]{1,0:T(8,128)(2,1)S(1)} %collective-permute-done.11.refs_0_, ...), custom_call_target="tpu_custom_call" | custom-call | flops 1073741824 | bytes 4097152 | tf_op jit(solution)/shard_map/pallas_call | solution.py:71
  53.0 10.4 %all_to_all.15.lse_all = f32[16,16,128]{2,1,0:T(8,128)S(1)} all-to-all(f32[16,16,128]{2,1,0:T(8,128)S(1)} %shard_map.55), channel_id=1, replica_groups=mesh['yl'=2,'x'=4,'yh'=2,'z'=4,'c'=2] {'yh','z','c'}, dimensions={0} | all-to-all | bytes 262144 | tf_op jit(solution)/shard_map/all_to_all | solution.py:337
  65.6 3.5 %shard_map.57 = (f32[2,136,512]{2,1,0:T(8,128)S(1)}, bf16[2,136,512]{2,1,0:T(8,128)(2,1)S(1)}, bf16[2,136,512]{2,1,0:T(8,128)(2,1)S(1)}, bf16[2,136,512]{2,1,0:T(8,128)(2,1)S(1)}, bf16[512,2048]{1,0:T(8,128)(2,1)S(1)}) custom-call(f32[16,128]{1,0:T(8,128)S(1)} %get-tuple-element.57.total, bf16[512,2048]{1,0:T(8,128)(2,1)S(1)} %get-tuple-element.58.resp1, ...), custom_call_target="tpu_custom_call" | custom-call | flops 2147483648 | bytes 8000000 | tf_op jit(solution)/shard_map/pallas_call | solution.py:71
  69.1 2.8 %collective-permute-start.15 = (bf16[2,136,512]{2,1,0:T(8,128)(2,1)S(1)}, bf16[2,136,512]{2,1,0:T(8,128)(2,1)S(1)}, u32[]{:S(2)}, u32[]{:S(2)}) collective-permute-start(bf16[2,136,512]{2,1,0:T(8,128)(2,1)S(1)} %get-tuple-element.60), channel_id=1, source_target_pairs={{0,32},{16,48},{32,0},{48,16},{1,33},{17,49},{33,1},{49,17},{2,34}... | collective-permute-start | bytes 835592 | tf_op jit(solution)/shard_map/ppermute | solution.py:61
  72.2 2.4 %collective-permute-start.17 = (bf16[2,136,512]{2,1,0:T(8,128)(2,1)S(1)}, bf16[2,136,512]{2,1,0:T(8,128)(2,1)S(1)}, u32[]{:S(2)}, u32[]{:S(2)}) collective-permute-start(bf16[2,136,512]{2,1,0:T(8,128)(2,1)S(1)} %get-tuple-element.62), channel_id=1, source_target_pairs={{0,48},{16,0},{32,16},{48,32},{1,49},{17,1},{33,17},{49,33},{2,50}... | collective-permute-start | bytes 835592 | tf_op jit(solution)/shard_map/ppermute | solution.py:61
  74.6 3.4 %collective-permute-done.15.got1 = bf16[2,136,512]{2,1,0:T(8,128)(2,1)S(1)} collective-permute-done((bf16[2,136,512]{2,1,0:T(8,128)(2,1)S(1)}, bf16[2,136,512]{2,1,0:T(8,128)(2,1)S(1)}, u32[]{:S(2)}, u32[]{:S(2)}) %collective-permute-start.15) | collective-permute-done | bytes 278560 | tf_op jit(solution)/shard_map/ppermute | solution.py:61
  78.0 7.2 %collective-permute-done.16.got2 = bf16[2,136,512]{2,1,0:T(8,128)(2,1)S(1)} collective-permute-done((bf16[2,136,512]{2,1,0:T(8,128)(2,1)S(1)}, bf16[2,136,512]{2,1,0:T(8,128)(2,1)S(1)}, u32[]{:S(2)}, u32[]{:S(2)}) %collective-permute-start.16) | collective-permute-done | bytes 278560 | tf_op jit(solution)/shard_map/ppermute | solution.py:61
  88.4 2.1 %collective-permute-start.21 = (bf16[128,512]{1,0:T(8,128)(2,1)S(1)}, bf16[128,512]{1,0:T(8,128)(2,1)S(1)}, u32[]{:S(2)}, u32[]{:S(2)}) collective-permute-start(bf16[128,512]{1,0:T(8,128)(2,1)S(1)} %get-tuple-element.69), channel_id=1, source_target_pairs={{0,16},{16,32},{32,48},{48,0},{1,17},{17,33},{33,49},{49,1},{2,18}... | collective-permute-start | bytes 393224 | tf_op jit(solution)/shard_map/ppermute | solution.py:61
  93.1 3.5 %collective-permute-done.21.refs_4_ = bf16[128,512]{1,0:T(8,128)(2,1)S(1)} collective-permute-done((bf16[128,512]{1,0:T(8,128)(2,1)S(1)}, bf16[128,512]{1,0:T(8,128)(2,1)S(1)}, u32[]{:S(2)}, u32[]{:S(2)}) %collective-permute-start.21) | collective-permute-done | bytes 131104 | tf_op jit(solution)/shard_map/ppermute | solution.py:61
  101.3 18.8 %all_to_all.16.parts = bf16[64,40,128]{2,1,0:T(8,128)(2,1)S(1)} all-to-all(bf16[64,40,128]{2,1,0:T(8,128)(2,1)S(1)} %shard_map.64), channel_id=1, replica_groups=mesh['yl'=2,'x'=4,'yh'=2,'z'=4,'c'=2] {'yl','x','yh','z'}, dimensions={0} | all-to-all | bytes 1310720 | tf_op jit(solution)/shard_map/all_to_all | solution.py:375
  121.1 5.5 %all-to-all-start.2 = ((bf16[64,32,128]{2,1,0:T(8,128)(2,1)}), bf16[64,32,128]{2,1,0:T(8,128)(2,1)S(1)}, u32[]{:S(2)}, u32[]{:S(2)}) async-start(bf16[64,32,128]{2,1,0:T(8,128)(2,1)} %shard_map.65), calls=%async_computation.2 | async-start | bytes 1048576 | tf_op jit(solution)/shard_map/all_to_all | solution.py:377
  126.6 2.8 %collective-permute-start.25 = (bf16[128,1024]{1,0:T(8,128)(2,1)S(1)}, bf16[128,1024]{1,0:T(8,128)(2,1)S(1)}, u32[]{:S(2)}, u32[]{:S(2)}) collective-permute-start(bf16[128,1024]{1,0:T(8,128)(2,1)S(1)} %get-tuple-element.73.refs_0_), channel_id=1, source_target_pairs={{0,32},{16,48},{32,0},{48,16},{1,33},{17,49},{33,1},{49,17},{2,34}... | collective-permute-start | bytes 786440 | tf_op jit(solution)/shard_map/ppermute | solution.py:61
  131.2 6.1 %all-to-all-done.2.mine = bf16[64,32,128]{2,1,0:T(8,128)(2,1)S(1)} async-done(((bf16[64,32,128]{2,1,0:T(8,128)(2,1)}), bf16[64,32,128]{2,1,0:T(8,128)(2,1)S(1)}, u32[]{:S(2)}, u32[]{:S(2)}) %all-to-all-start.2) | async-done | bytes 524320 | tf_op jit(solution)/shard_map/all_to_all | solution.py:377
  137.3 6.6 %collective-permute-start.31 = (bf16[64,32,128]{2,1,0:T(8,128)(2,1)S(1)}, bf16[64,32,128]{2,1,0:T(8,128)(2,1)S(1)}, u32[]{:S(2)}, u32[]{:S(2)}) collective-permute-start(bf16[64,32,128]{2,1,0:T(8,128)(2,1)S(1)} %all-to-all-done.2.mine), channel_id=1, source_target_pairs={{0,1},{1,0},{2,3},{3,2},{4,5},{5,4},{6,7},{7,6},{8,9},{9,8},{10,11... | collective-permute-start | bytes 1572872 | tf_op jit(solution)/shard_map/ppermute | solution.py:61
  146.6 5.1 %collective-permute-done.28.refs_1_ = bf16[128,1024]{1,0:T(8,128)(2,1)S(1)} collective-permute-done((bf16[128,1024]{1,0:T(8,128)(2,1)S(1)}, bf16[128,1024]{1,0:T(8,128)(2,1)S(1)}, u32[]{:S(2)}, u32[]{:S(2)}) %collective-permute-start.28) | collective-permute-done | bytes 262176 | tf_op jit(solution)/shard_map/ppermute | solution.py:61
  153.1 4.2 %collective-permute-done.24.refs_1_ = bf16[128,1024]{1,0:T(8,128)(2,1)S(1)} collective-permute-done((bf16[128,1024]{1,0:T(8,128)(2,1)S(1)}, bf16[128,1024]{1,0:T(8,128)(2,1)S(1)}, u32[]{:S(2)}, u32[]{:S(2)}) %collective-permute-start.24) | collective-permute-done | bytes 262176 | tf_op jit(solution)/shard_map/ppermute | solution.py:61
  (73 shorter events, 36.5 us)
Async XLA Ops:
  0.6 10.3 %collective-permute-start.5 = (bf16[128,1024]{1,0:T(8,128)(2,1)}, bf16[128,1024]{1,0:T(8,128)(2,1)S(1)}, u32[]{:S(2)}, u32[]{:S(2)}) collective-permute-start(bf16[128,1024]{1,0:T(8,128)(2,1)} %refs_0_.1), channel_id=1, source_target_pairs={{0,6},{2,0},{4,2},{6,4},{1,7},{3,1},{5,3},{7,5},{8,14},{10,8},{12,... | collective-permute-start | bytes 786440 | tf_op jit(solution)/shard_map/ppermute | solution.py:61
  8.2 15.0 %collective-permute-start.3 = (bf16[128,1024]{1,0:T(8,128)(2,1)}, bf16[128,1024]{1,0:T(8,128)(2,1)S(1)}, u32[]{:S(2)}, u32[]{:S(2)}) collective-permute-start(bf16[128,1024]{1,0:T(8,128)(2,1)} %refs_0_.1), channel_id=1, source_target_pairs={{0,2},{2,4},{4,6},{6,0},{1,3},{3,5},{5,7},{7,1},{8,10},{10,12},{12... | collective-permute-start | bytes 786440 | tf_op jit(solution)/shard_map/ppermute | solution.py:61
  8.2 15.0 %collective-permute-start.9 = (bf16[128,1024]{1,0:T(8,128)(2,1)}, bf16[128,1024]{1,0:T(8,128)(2,1)S(1)}, u32[]{:S(2)}, u32[]{:S(2)}) collective-permute-start(bf16[128,1024]{1,0:T(8,128)(2,1)} %refs_0_.1), channel_id=1, source_target_pairs={{0,12},{2,14},{4,8},{6,10},{8,4},{10,6},{12,0},{14,2},{1,13},{3,15... | collective-permute-start | bytes 786440 | tf_op jit(solution)/shard_map/ppermute | solution.py:61
  9.3 21.2 %collective-permute-start.7 = (bf16[128,1024]{1,0:T(8,128)(2,1)}, bf16[128,1024]{1,0:T(8,128)(2,1)S(1)}, u32[]{:S(2)}, u32[]{:S(2)}) collective-permute-start(bf16[128,1024]{1,0:T(8,128)(2,1)} %refs_0_.1), channel_id=1, source_target_pairs={{0,4},{2,6},{4,0},{6,2},{1,5},{3,7},{5,1},{7,3},{8,12},{10,14},{12... | collective-permute-start | bytes 786440 | tf_op jit(solution)/shard_map/ppermute | solution.py:61
  10.9 19.6 %collective-permute-start.6 = (bf16[128,1024]{1,0:T(8,128)(2,1)S(1)}, bf16[128,1024]{1,0:T(8,128)(2,1)S(1)}, u32[]{:S(2)}, u32[]{:S(2)}) collective-permute-start(bf16[128,1024]{1,0:T(8,128)(2,1)S(1)} %collective-permute-done.5.refs_2_), channel_id=1, source_target_pairs={{0,1},{1,0},{2,3},{3,2},{4,5},{5,4},{6,7},{7,6},{8,9},{9,8},{10,11... | collective-permute-start | bytes 786440 | tf_op jit(solution)/shard_map/ppermute | solution.py:61
  13.9 17.0 %collective-permute-start.13 = (bf16[128,1024]{1,0:T(8,128)(2,1)S(1)}, bf16[128,1024]{1,0:T(8,128)(2,1)S(1)}, u32[]{:S(2)}, u32[]{:S(2)}) collective-permute-start(bf16[128,1024]{1,0:T(8,128)(2,1)S(1)} %collective-permute-done.1.refs_2_), channel_id=1, source_target_pairs={{0,6},{2,0},{4,2},{6,4},{1,7},{3,1},{5,3},{7,5},{8,14},{10,8},{12,... | collective-permute-start | bytes 786440 | tf_op jit(solution)/shard_map/ppermute | solution.py:61
  23.2 19.2 %collective-permute-start.10 = (bf16[128,1024]{1,0:T(8,128)(2,1)S(1)}, bf16[128,1024]{1,0:T(8,128)(2,1)S(1)}, u32[]{:S(2)}, u32[]{:S(2)}) collective-permute-start(bf16[128,1024]{1,0:T(8,128)(2,1)S(1)} %collective-permute-done.9.refs_2_), channel_id=1, source_target_pairs={{0,1},{1,0},{2,3},{3,2},{4,5},{5,4},{6,7},{7,6},{8,9},{9,8},{10,11... | collective-permute-start | bytes 786440 | tf_op jit(solution)/shard_map/ppermute | solution.py:61
  30.4 12.1 %collective-permute-start.8 = (bf16[128,1024]{1,0:T(8,128)(2,1)S(1)}, bf16[128,1024]{1,0:T(8,128)(2,1)S(1)}, u32[]{:S(2)}, u32[]{:S(2)}) collective-permute-start(bf16[128,1024]{1,0:T(8,128)(2,1)S(1)} %collective-permute-done.7.refs_0_), channel_id=1, source_target_pairs={{0,1},{1,0},{2,3},{3,2},{4,5},{5,4},{6,7},{7,6},{8,9},{9,8},{10,11... | collective-permute-start | bytes 786440 | tf_op jit(solution)/shard_map/ppermute | solution.py:61
  30.5 16.9 %collective-permute-start.4 = (bf16[128,1024]{1,0:T(8,128)(2,1)S(1)}, bf16[128,1024]{1,0:T(8,128)(2,1)S(1)}, u32[]{:S(2)}, u32[]{:S(2)}) collective-permute-start(bf16[128,1024]{1,0:T(8,128)(2,1)S(1)} %collective-permute-done.3.refs_0_), channel_id=1, source_target_pairs={{0,1},{1,0},{2,3},{3,2},{4,5},{5,4},{6,7},{7,6},{8,9},{9,8},{10,11... | collective-permute-start | bytes 786440 | tf_op jit(solution)/shard_map/ppermute | solution.py:61
  30.9 18.3 %collective-permute-start = (bf16[128,1024]{1,0:T(8,128)(2,1)}, bf16[128,1024]{1,0:T(8,128)(2,1)S(1)}, u32[]{:S(2)}, u32[]{:S(2)}) collective-permute-start(bf16[128,1024]{1,0:T(8,128)(2,1)} %refs_0_.1), channel_id=1, source_target_pairs={{0,1},{1,0},{2,3},{3,2},{4,5},{5,4},{6,7},{7,6},{8,9},{9,8},{10,11... | collective-permute-start | bytes 786440 | tf_op jit(solution)/shard_map/ppermute | solution.py:61
  31.7 17.6 %collective-permute-start.2 = (bf16[128,1024]{1,0:T(8,128)(2,1)S(1)}, bf16[128,1024]{1,0:T(8,128)(2,1)S(1)}, u32[]{:S(2)}, u32[]{:S(2)}) collective-permute-start(bf16[128,1024]{1,0:T(8,128)(2,1)S(1)} %collective-permute-done.1.refs_2_), channel_id=1, source_target_pairs={{0,1},{1,0},{2,3},{3,2},{4,5},{5,4},{6,7},{7,6},{8,9},{9,8},{10,11... | collective-permute-start | bytes 786440 | tf_op jit(solution)/shard_map/ppermute | solution.py:61
  42.4 8.7 %collective-permute-start.14 = (bf16[128,1024]{1,0:T(8,128)(2,1)S(1)}, bf16[128,1024]{1,0:T(8,128)(2,1)S(1)}, u32[]{:S(2)}, u32[]{:S(2)}) collective-permute-start(bf16[128,1024]{1,0:T(8,128)(2,1)S(1)} %collective-permute-done.13.refs_2_), channel_id=1, source_target_pairs={{0,1},{1,0},{2,3},{3,2},{4,5},{5,4},{6,7},{7,6},{8,9},{9,8},{10,11... | collective-permute-start | bytes 786440 | tf_op jit(solution)/shard_map/ppermute | solution.py:61
  64.7 21.4 %collective-permute-start.19 = (bf16[512,512]{1,0:T(8,128)(2,1)S(1)}, bf16[512,512]{1,0:T(8,128)(2,1)S(1)}, u32[]{:S(2)}, u32[]{:S(2)}) collective-permute-start(bf16[512,512]{1,0:T(8,128)(2,1)S(1)} %get-tuple-element.66), channel_id=1, source_target_pairs={{0,64},{64,0},{1,65},{65,1},{2,66},{66,2},{3,67},{67,3},{4,68},{68... | collective-permute-start | bytes 1572872 | tf_op jit(solution)/shard_map/ppermute | solution.py:61
  69.1 8.9 %collective-permute-start.15 = (bf16[2,136,512]{2,1,0:T(8,128)(2,1)S(1)}, bf16[2,136,512]{2,1,0:T(8,128)(2,1)S(1)}, u32[]{:S(2)}, u32[]{:S(2)}) collective-permute-start(bf16[2,136,512]{2,1,0:T(8,128)(2,1)S(1)} %get-tuple-element.60), channel_id=1, source_target_pairs={{0,32},{16,48},{32,0},{48,16},{1,33},{17,49},{33,1},{49,17},{2,34}... | collective-permute-start | bytes 835592 | tf_op jit(solution)/shard_map/ppermute | solution.py:61
  71.9 13.3 %collective-permute-start.16 = (bf16[2,136,512]{2,1,0:T(8,128)(2,1)S(1)}, bf16[2,136,512]{2,1,0:T(8,128)(2,1)S(1)}, u32[]{:S(2)}, u32[]{:S(2)}) collective-permute-start(bf16[2,136,512]{2,1,0:T(8,128)(2,1)S(1)} %get-tuple-element.61), channel_id=1, source_target_pairs={{0,16},{16,32},{32,48},{48,0},{1,17},{17,33},{33,49},{49,1},{2,18}... | collective-permute-start | bytes 835592 | tf_op jit(solution)/shard_map/ppermute | solution.py:61
  72.2 13.0 %collective-permute-start.17 = (bf16[2,136,512]{2,1,0:T(8,128)(2,1)S(1)}, bf16[2,136,512]{2,1,0:T(8,128)(2,1)S(1)}, u32[]{:S(2)}, u32[]{:S(2)}) collective-permute-start(bf16[2,136,512]{2,1,0:T(8,128)(2,1)S(1)} %get-tuple-element.62), channel_id=1, source_target_pairs={{0,48},{16,0},{32,16},{48,32},{1,49},{17,1},{33,17},{49,33},{2,50}... | collective-permute-start | bytes 835592 | tf_op jit(solution)/shard_map/ppermute | solution.py:61
  121.1 16.2 %all-to-all-start.2 = ((bf16[64,32,128]{2,1,0:T(8,128)(2,1)}), bf16[64,32,128]{2,1,0:T(8,128)(2,1)S(1)}, u32[]{:S(2)}, u32[]{:S(2)}) async-start(bf16[64,32,128]{2,1,0:T(8,128)(2,1)} %shard_map.65), calls=%async_computation.2 | async-start | bytes 1048576 | tf_op jit(solution)/shard_map/all_to_all | solution.py:377
  126.6 17.2 %collective-permute-start.25 = (bf16[128,1024]{1,0:T(8,128)(2,1)S(1)}, bf16[128,1024]{1,0:T(8,128)(2,1)S(1)}, u32[]{:S(2)}, u32[]{:S(2)}) collective-permute-start(bf16[128,1024]{1,0:T(8,128)(2,1)S(1)} %get-tuple-element.73.refs_0_), channel_id=1, source_target_pairs={{0,32},{16,48},{32,0},{48,16},{1,33},{17,49},{33,1},{49,17},{2,34}... | collective-permute-start | bytes 786440 | tf_op jit(solution)/shard_map/ppermute | solution.py:61
  129.5 14.4 %collective-permute-start.23 = (bf16[128,1024]{1,0:T(8,128)(2,1)S(1)}, bf16[128,1024]{1,0:T(8,128)(2,1)S(1)}, u32[]{:S(2)}, u32[]{:S(2)}) collective-permute-start(bf16[128,1024]{1,0:T(8,128)(2,1)S(1)} %get-tuple-element.73.refs_0_), channel_id=1, source_target_pairs={{0,64},{64,0},{1,65},{65,1},{2,66},{66,2},{3,67},{67,3},{4,68},{68... | collective-permute-start | bytes 786440 | tf_op jit(solution)/shard_map/ppermute | solution.py:61
  130.8 15.4 %collective-permute-start.29 = (bf16[128,1024]{1,0:T(8,128)(2,1)S(1)}, bf16[128,1024]{1,0:T(8,128)(2,1)S(1)}, u32[]{:S(2)}, u32[]{:S(2)}) collective-permute-start(bf16[128,1024]{1,0:T(8,128)(2,1)S(1)} %get-tuple-element.73.refs_0_), channel_id=1, source_target_pairs={{0,16},{16,32},{32,48},{48,0},{1,17},{17,33},{33,49},{49,1},{2,18}... | collective-permute-start | bytes 786440 | tf_op jit(solution)/shard_map/ppermute | solution.py:61
  137.3 21.4 %collective-permute-start.31 = (bf16[64,32,128]{2,1,0:T(8,128)(2,1)S(1)}, bf16[64,32,128]{2,1,0:T(8,128)(2,1)S(1)}, u32[]{:S(2)}, u32[]{:S(2)}) collective-permute-start(bf16[64,32,128]{2,1,0:T(8,128)(2,1)S(1)} %all-to-all-done.2.mine), channel_id=1, source_target_pairs={{0,1},{1,0},{2,3},{3,2},{4,5},{5,4},{6,7},{7,6},{8,9},{9,8},{10,11... | collective-permute-start | bytes 1572872 | tf_op jit(solution)/shard_map/ppermute | solution.py:61
  143.9 9.2 %collective-permute-start.26 = (bf16[128,1024]{1,0:T(8,128)(2,1)S(1)}, bf16[128,1024]{1,0:T(8,128)(2,1)S(1)}, u32[]{:S(2)}, u32[]{:S(2)}) collective-permute-start(bf16[128,1024]{1,0:T(8,128)(2,1)S(1)} %collective-permute-done.25.refs_2_), channel_id=1, source_target_pairs={{0,64},{64,0},{1,65},{65,1},{2,66},{66,2},{3,67},{67,3},{4,68},{68... | collective-permute-start | bytes 786440 | tf_op jit(solution)/shard_map/ppermute | solution.py:61
  143.9 9.2 %collective-permute-start.27 = (bf16[128,1024]{1,0:T(8,128)(2,1)S(1)}, bf16[128,1024]{1,0:T(8,128)(2,1)S(1)}, u32[]{:S(2)}, u32[]{:S(2)}) collective-permute-start(bf16[128,1024]{1,0:T(8,128)(2,1)S(1)} %collective-permute-done.23.refs_0_), channel_id=1, source_target_pairs={{0,16},{16,32},{32,48},{48,0},{1,17},{17,33},{33,49},{49,1},{2,18}... | collective-permute-start | bytes 786440 | tf_op jit(solution)/shard_map/ppermute | solution.py:61
  146.3 11.1 %collective-permute-start.24 = (bf16[128,1024]{1,0:T(8,128)(2,1)S(1)}, bf16[128,1024]{1,0:T(8,128)(2,1)S(1)}, u32[]{:S(2)}, u32[]{:S(2)}) collective-permute-start(bf16[128,1024]{1,0:T(8,128)(2,1)S(1)} %collective-permute-done.23.refs_0_), channel_id=1, source_target_pairs={{0,48},{16,0},{32,16},{48,32},{1,49},{17,1},{33,17},{49,33},{2,50}... | collective-permute-start | bytes 786440 | tf_op jit(solution)/shard_map/ppermute | solution.py:61
  (15 other events, 83.0 us)

commit v3 on v2

--- a/solution.py
+++ b/solution.py
@@ -26,8 +26,8 @@
 CHUNKS = (
     ((0, 0, 0), (0, 0, 1), (1, 0, 0), (1, 0, 1)),
     ((0, 1, 0), (0, 1, 1), (0, 3, 0), (0, 3, 1)),
+    ((1, 1, 0), (1, 1, 1), (1, 3, 0), (1, 3, 1)),
     ((0, 2, 0), (0, 2, 1), (1, 2, 0), (1, 2, 1)),
-    ((1, 1, 0), (1, 1, 1), (1, 3, 0), (1, 3, 1)),
 )
 PIECES = tuple(p for chunk in CHUNKS for p in chunk)
 NP = len(PIECES)
@@ -300,7 +300,7 @@
     down = sent(embeds, "z", 3)
     across = sent(embeds, "yh", 1)
     far = sent(embeds, "z", 2)
-    corner = moved(embeds, ("yh", "z"), (1, 2))
+    corner = sent(far, "yh", 1)
     across_up = sent(across, "z", 1)
     across_down = sent(across, "z", 3)
 
@@ -310,15 +310,16 @@
             both += [x, sent(x, "c", 1)]
         return both
 
+    fine, coarse = (pltpu.with_memory_space_constraint(a, pltpu.HBM) for a in (fine, coarse))
     fine, coarse, fine_sq, coarse_sq = call(
         norms_kernel, (fine, coarse),
         [sds((1024, 1024), BF16), sds((512, 1024), BF16), sds((1024, 1), F32), sds((512, 1), F32)],
-        in_specs=[FAR, FAR], scratch=[pltpu.SemaphoreType.DMA((12,))], limit=60, flops=3_000_000, moved_bytes=3_000_000,
+        in_specs=[FAR, FAR], scratch=[pltpu.SemaphoreType.DMA((12,))], limit=16, flops=3_000_000, moved_bytes=3_000_000,
     )
 
     inputs = (
         with_twin(own=embeds, across=across), with_twin(up=up, down=down),
-        with_twin(far=far, corner=corner), with_twin(across_up=across_up, across_down=across_down),
+        with_twin(across_up=across_up, across_down=across_down), with_twin(far=far, corner=corner),
     )
     probs, peaks, lses, chunks = [], [], [], []
     for blocks in inputs:

time: 161 us -> 149 us (0.925)
  starting transfers between devices: 59.2 us -> 53.4 us
  waiting for transfers between devices: 42.4 us -> 38.5 us
  blocking collectives: 29.1 us -> 32 us
  local copies, waits for them, and re-layouts: 2.65 us -> 0.01 us
  Pallas kernels: 25.9 us -> 24.1 us
    ppermute x32, starting transfers between devices: 53.6 us -> 47.8 us  [moved(): return lax.ppermute(x, axes, perm)]
    ppermute x32, waiting for transfers between devices: 36.3 us -> 32.4 us  [moved(): return lax.ppermute(x, axes, perm)]
    all_to_all x1, blocking collectives: 10.4 us -> 13.7 us  [step(): lse_all = lax.all_to_all(table, INNER, 0, 0, tiled=True)]
    unnamed x12 -> x2, local copies, waits for them, and re-layouts: 2.65 us -> 0.01 us
    pallas_call x17, Pallas kernels: 25.9 us -> 24.1 us  [call(): pl.pallas_call(kernel, in_specs=in_specs or [INSIDE] * len(ins), out_spec...]
  transfers between devices with their start and end apart: 33 -> 33, of which waited for: 12 -> 11; matrix products, arithmetic and copies ran while one was open for 0% -> 0% of each run, Pallas kernels for 12% -> 11%
where the time goes in v3:
time: 149 us
  starting transfers between devices  53.4 us (36%)
  waiting for transfers between devices  38.5 us (26%)
  blocking collectives  32 us (21%)
  Pallas kernels  24.1 us (16%)
    ppermute x32, starting transfers between devices, moved(): return lax.ppermute(x, axes, perm)  47.8 us
    ppermute x32, waiting for transfers between devices, moved(): return lax.ppermute(x, axes, perm)  32.4 us
    pallas_call x17, Pallas kernels, call(): pl.pallas_call(kernel, in_specs=in_specs or [INSIDE] * len(ins), out_spec...  24.1 us
    all_to_all x1, blocking collectives, step(): parts = lax.all_to_all(half, CHIPS, 0, 0, tiled=True)  18.4 us
    all_to_all x1, blocking collectives, step(): lse_all = lax.all_to_all(table, INNER, 0, 0, tiled=True)  13.7 us
    all_to_all x1, waiting for transfers between devices, step(): mine_new = lax.all_to_all(new, CHIPS, 0, 0, tiled=True)  6.1 us
    all_to_all x1, starting transfers between devices, step(): mine_new = lax.all_to_all(new, CHIPS, 0, 0, tiled=True)  5.54 us
  transfers between devices with their start and end apart: 33, of which 11 were waited for; matrix products, arithmetic and copies ran while one was open for 0% of the time, Pallas kernels for 11%

profile of v3, /device:TPU:1, one launch (start us, length us, event | category | flops | bytes accessed | tf_op | source)
XLA Modules:
  0.0 149.0 jit_solution(2624893026779006322)
XLA Ops:
  0.6 2.5 %collective-permute-start.3 = (bf16[128,1024]{1,0:T(8,128)(2,1)}, bf16[128,1024]{1,0:T(8,128)(2,1)S(1)}, u32[]{:S(2)}, u32[]{:S(2)}) collective-permute-start(bf16[128,1024]{1,0:T(8,128)(2,1)} %refs_0_.1), channel_id=1, source_target_pairs={{0,2},{2,4},{4,6},{6,0},{1,3},{3,5},{5,7},{7,1},{8,10},{10,12},{12... | collective-permute-start | bytes 786440 | tf_op jit(solution)/shard_map/ppermute | solution.py:61
  3.2 2.9 %collective-permute-start.1 = (bf16[128,1024]{1,0:T(8,128)(2,1)}, bf16[128,1024]{1,0:T(8,128)(2,1)S(1)}, u32[]{:S(2)}, u32[]{:S(2)}) collective-permute-start(bf16[128,1024]{1,0:T(8,128)(2,1)} %refs_0_.1), channel_id=1, source_target_pairs={{0,8},{8,0},{1,9},{9,1},{2,10},{10,2},{3,11},{11,3},{4,12},{12,4},... | collective-permute-start | bytes 786440 | tf_op jit(solution)/shard_map/ppermute | solution.py:61
  6.1 3.3 %collective-permute-start.11 = (bf16[128,1024]{1,0:T(8,128)(2,1)}, bf16[128,1024]{1,0:T(8,128)(2,1)S(1)}, u32[]{:S(2)}, u32[]{:S(2)}) collective-permute-start(bf16[128,1024]{1,0:T(8,128)(2,1)} %refs_0_.1), channel_id=1, source_target_pairs={{0,4},{2,6},{4,0},{6,2},{1,5},{3,7},{5,1},{7,3},{8,12},{10,14},{12... | collective-permute-start | bytes 786440 | tf_op jit(solution)/shard_map/ppermute | solution.py:61
  12.8 2.6 %collective-permute-start.9 = (bf16[128,1024]{1,0:T(8,128)(2,1)S(1)}, bf16[128,1024]{1,0:T(8,128)(2,1)S(1)}, u32[]{:S(2)}, u32[]{:S(2)}) collective-permute-start(bf16[128,1024]{1,0:T(8,128)(2,1)S(1)} %collective-permute-done.1.refs_2_), channel_id=1, source_target_pairs={{0,6},{2,0},{4,2},{6,4},{1,7},{3,1},{5,3},{7,5},{8,14},{10,8},{12,... | collective-permute-start | bytes 786440 | tf_op jit(solution)/shard_map/ppermute | solution.py:61
  15.3 2.7 %collective-permute-done.11.refs_0_ = bf16[128,1024]{1,0:T(8,128)(2,1)S(1)} collective-permute-done((bf16[128,1024]{1,0:T(8,128)(2,1)}, bf16[128,1024]{1,0:T(8,128)(2,1)S(1)}, u32[]{:S(2)}, u32[]{:S(2)}) %collective-permute-start.11) | collective-permute-done | bytes 262176 | tf_op jit(solution)/shard_map/ppermute | solution.py:61
  18.0 2.9 %collective-permute-start.13 = (bf16[128,1024]{1,0:T(8,128)(2,1)S(1)}, bf16[128,1024]{1,0:T(8,128)(2,1)S(1)}, u32[]{:S(2)}, u32[]{:S(2)}) collective-permute-start(bf16[128,1024]{1,0:T(8,128)(2,1)S(1)} %collective-permute-done.11.refs_0_), channel_id=1, source_target_pairs={{0,8},{8,0},{1,9},{9,1},{2,10},{10,2},{3,11},{11,3},{4,12},{12,4},... | collective-permute-start | bytes 786440 | tf_op jit(solution)/shard_map/ppermute | solution.py:61
  20.9 2.4 %collective-permute-start.6 = (bf16[128,1024]{1,0:T(8,128)(2,1)S(1)}, bf16[128,1024]{1,0:T(8,128)(2,1)S(1)}, u32[]{:S(2)}, u32[]{:S(2)}) collective-permute-start(bf16[128,1024]{1,0:T(8,128)(2,1)S(1)} %collective-permute-done.5.refs_2_), channel_id=1, source_target_pairs={{0,1},{1,0},{2,3},{3,2},{4,5},{5,4},{6,7},{7,6},{8,9},{9,8},{10,11... | collective-permute-start | bytes 786440 | tf_op jit(solution)/shard_map/ppermute | solution.py:61
  23.4 2.7 %collective-permute-done.9.refs_2_ = bf16[128,1024]{1,0:T(8,128)(2,1)S(1)} collective-permute-done((bf16[128,1024]{1,0:T(8,128)(2,1)S(1)}, bf16[128,1024]{1,0:T(8,128)(2,1)S(1)}, u32[]{:S(2)}, u32[]{:S(2)}) %collective-permute-start.9) | collective-permute-done | bytes 262176 | tf_op jit(solution)/shard_map/ppermute | solution.py:61
  28.2 2.6 %shard_map.50 = (bf16[1024,1024]{1,0:T(8,128)(2,1)S(1)}, bf16[512,1024]{1,0:T(8,128)(2,1)S(1)}, f32[1024,1]{1,0:T(8,128)S(1)}, f32[512,1]{1,0:T(8,128)S(1)}) custom-call(bf16[1024,1024]{1,0:T(8,128)(2,1)} %fine_hbm.1, bf16[512,1024]{1,0:T(8,128)(2,1)} %coarse_hbm.1), custom_call_target="tpu_custom_call" | custom-call | flops 3000000 | bytes 3000000 | tf_op jit(solution)/shard_map/pallas_call | solution.py:71
  38.8 13.7 %all_to_all.15.lse_all = f32[16,16,128]{2,1,0:T(8,128)S(1)} all-to-all(f32[16,16,128]{2,1,0:T(8,128)S(1)} %shard_map.55), channel_id=1, replica_groups=mesh['yl'=2,'x'=4,'yh'=2,'z'=4,'c'=2] {'yh','z','c'}, dimensions={0} | all-to-all | bytes 262144 | tf_op jit(solution)/shard_map/all_to_all | solution.py:338
  54.3 3.5 %shard_map.57 = (f32[2,136,512]{2,1,0:T(8,128)S(1)}, bf16[2,136,512]{2,1,0:T(8,128)(2,1)S(1)}, bf16[2,136,512]{2,1,0:T(8,128)(2,1)S(1)}, bf16[2,136,512]{2,1,0:T(8,128)(2,1)S(1)}, bf16[512,2048]{1,0:T(8,128)(2,1)S(1)}) custom-call(f32[16,128]{1,0:T(8,128)S(1)} %get-tuple-element.57.total, bf16[512,2048]{1,0:T(8,128)(2,1)S(1)} %get-tuple-element.58.resp1, ...), custom_call_target="tpu_custom_call" | custom-call | flops 2147483648 | bytes 8000000 | tf_op jit(solution)/shard_map/pallas_call | solution.py:71
  57.8 2.8 %collective-permute-start.15 = (bf16[2,136,512]{2,1,0:T(8,128)(2,1)S(1)}, bf16[2,136,512]{2,1,0:T(8,128)(2,1)S(1)}, u32[]{:S(2)}, u32[]{:S(2)}) collective-permute-start(bf16[2,136,512]{2,1,0:T(8,128)(2,1)S(1)} %get-tuple-element.60), channel_id=1, source_target_pairs={{0,32},{16,48},{32,0},{48,16},{1,33},{17,49},{33,1},{49,17},{2,34}... | collective-permute-start | bytes 835592 | tf_op jit(solution)/shard_map/ppermute | solution.py:61
  60.9 2.4 %collective-permute-start.17 = (bf16[2,136,512]{2,1,0:T(8,128)(2,1)S(1)}, bf16[2,136,512]{2,1,0:T(8,128)(2,1)S(1)}, u32[]{:S(2)}, u32[]{:S(2)}) collective-permute-start(bf16[2,136,512]{2,1,0:T(8,128)(2,1)S(1)} %get-tuple-element.62), channel_id=1, source_target_pairs={{0,48},{16,0},{32,16},{48,32},{1,49},{17,1},{33,17},{49,33},{2,50}... | collective-permute-start | bytes 835592 | tf_op jit(solution)/shard_map/ppermute | solution.py:61
  63.3 3.4 %collective-permute-done.15.got1 = bf16[2,136,512]{2,1,0:T(8,128)(2,1)S(1)} collective-permute-done((bf16[2,136,512]{2,1,0:T(8,128)(2,1)S(1)}, bf16[2,136,512]{2,1,0:T(8,128)(2,1)S(1)}, u32[]{:S(2)}, u32[]{:S(2)}) %collective-permute-start.15) | collective-permute-done | bytes 278560 | tf_op jit(solution)/shard_map/ppermute | solution.py:61
  66.7 7.2 %collective-permute-done.16.got2 = bf16[2,136,512]{2,1,0:T(8,128)(2,1)S(1)} collective-permute-done((bf16[2,136,512]{2,1,0:T(8,128)(2,1)S(1)}, bf16[2,136,512]{2,1,0:T(8,128)(2,1)S(1)}, u32[]{:S(2)}, u32[]{:S(2)}) %collective-permute-start.16) | collective-permute-done | bytes 278560 | tf_op jit(solution)/shard_map/ppermute | solution.py:61
  77.6 2.0 %collective-permute-start.21 = (bf16[128,512]{1,0:T(8,128)(2,1)S(1)}, bf16[128,512]{1,0:T(8,128)(2,1)S(1)}, u32[]{:S(2)}, u32[]{:S(2)}) collective-permute-start(bf16[128,512]{1,0:T(8,128)(2,1)S(1)} %get-tuple-element.69), channel_id=1, source_target_pairs={{0,16},{16,32},{32,48},{48,0},{1,17},{17,33},{33,49},{49,1},{2,18}... | collective-permute-start | bytes 393224 | tf_op jit(solution)/shard_map/ppermute | solution.py:61
  82.2 3.5 %collective-permute-done.21.refs_4_ = bf16[128,512]{1,0:T(8,128)(2,1)S(1)} collective-permute-done((bf16[128,512]{1,0:T(8,128)(2,1)S(1)}, bf16[128,512]{1,0:T(8,128)(2,1)S(1)}, u32[]{:S(2)}, u32[]{:S(2)}) %collective-permute-start.21) | collective-permute-done | bytes 131104 | tf_op jit(solution)/shard_map/ppermute | solution.py:61
  90.5 18.4 %all_to_all.16.parts = bf16[64,40,128]{2,1,0:T(8,128)(2,1)S(1)} all-to-all(bf16[64,40,128]{2,1,0:T(8,128)(2,1)S(1)} %shard_map.64), channel_id=1, replica_groups=mesh['yl'=2,'x'=4,'yh'=2,'z'=4,'c'=2] {'yl','x','yh','z'}, dimensions={0} | all-to-all | bytes 1310720 | tf_op jit(solution)/shard_map/all_to_all | solution.py:376
  109.8 5.5 %all-to-all-start.2 = ((bf16[64,32,128]{2,1,0:T(8,128)(2,1)}), bf16[64,32,128]{2,1,0:T(8,128)(2,1)S(1)}, u32[]{:S(2)}, u32[]{:S(2)}) async-start(bf16[64,32,128]{2,1,0:T(8,128)(2,1)} %shard_map.65), calls=%async_computation.2 | async-start | bytes 1048576 | tf_op jit(solution)/shard_map/all_to_all | solution.py:378
  115.3 2.8 %collective-permute-start.25 = (bf16[128,1024]{1,0:T(8,128)(2,1)S(1)}, bf16[128,1024]{1,0:T(8,128)(2,1)S(1)}, u32[]{:S(2)}, u32[]{:S(2)}) collective-permute-start(bf16[128,1024]{1,0:T(8,128)(2,1)S(1)} %get-tuple-element.73.refs_0_), channel_id=1, source_target_pairs={{0,32},{16,48},{32,0},{48,16},{1,33},{17,49},{33,1},{49,17},{2,34}... | collective-permute-start | bytes 786440 | tf_op jit(solution)/shard_map/ppermute | solution.py:61
  119.9 6.1 %all-to-all-done.2.mine = bf16[64,32,128]{2,1,0:T(8,128)(2,1)S(1)} async-done(((bf16[64,32,128]{2,1,0:T(8,128)(2,1)}), bf16[64,32,128]{2,1,0:T(8,128)(2,1)S(1)}, u32[]{:S(2)}, u32[]{:S(2)}) %all-to-all-start.2) | async-done | bytes 524320 | tf_op jit(solution)/shard_map/all_to_all | solution.py:378
  126.0 6.6 %collective-permute-start.31 = (bf16[64,32,128]{2,1,0:T(8,128)(2,1)S(1)}, bf16[64,32,128]{2,1,0:T(8,128)(2,1)S(1)}, u32[]{:S(2)}, u32[]{:S(2)}) collective-permute-start(bf16[64,32,128]{2,1,0:T(8,128)(2,1)S(1)} %all-to-all-done.2.mine), channel_id=1, source_target_pairs={{0,1},{1,0},{2,3},{3,2},{4,5},{5,4},{6,7},{7,6},{8,9},{9,8},{10,11... | collective-permute-start | bytes 1572872 | tf_op jit(solution)/shard_map/ppermute | solution.py:61
  135.3 5.1 %collective-permute-done.28.refs_1_ = bf16[128,1024]{1,0:T(8,128)(2,1)S(1)} collective-permute-done((bf16[128,1024]{1,0:T(8,128)(2,1)S(1)}, bf16[128,1024]{1,0:T(8,128)(2,1)S(1)}, u32[]{:S(2)}, u32[]{:S(2)}) %collective-permute-start.28) | collective-permute-done | bytes 262176 | tf_op jit(solution)/shard_map/ppermute | solution.py:61
  141.8 4.2 %collective-permute-done.24.refs_1_ = bf16[128,1024]{1,0:T(8,128)(2,1)S(1)} collective-permute-done((bf16[128,1024]{1,0:T(8,128)(2,1)S(1)}, bf16[128,1024]{1,0:T(8,128)(2,1)S(1)}, u32[]{:S(2)}, u32[]{:S(2)}) %collective-permute-start.24) | collective-permute-done | bytes 262176 | tf_op jit(solution)/shard_map/ppermute | solution.py:61
  (63 shorter events, 36.1 us)
Async XLA Ops:
  0.6 11.0 %collective-permute-start.3 = (bf16[128,1024]{1,0:T(8,128)(2,1)}, bf16[128,1024]{1,0:T(8,128)(2,1)S(1)}, u32[]{:S(2)}, u32[]{:S(2)}) collective-permute-start(bf16[128,1024]{1,0:T(8,128)(2,1)} %refs_0_.1), channel_id=1, source_target_pairs={{0,2},{2,4},{4,6},{6,0},{1,3},{3,5},{5,7},{7,1},{8,10},{10,12},{12... | collective-permute-start | bytes 786440 | tf_op jit(solution)/shard_map/ppermute | solution.py:61
  3.2 9.6 %collective-permute-start.1 = (bf16[128,1024]{1,0:T(8,128)(2,1)}, bf16[128,1024]{1,0:T(8,128)(2,1)S(1)}, u32[]{:S(2)}, u32[]{:S(2)}) collective-permute-start(bf16[128,1024]{1,0:T(8,128)(2,1)} %refs_0_.1), channel_id=1, source_target_pairs={{0,8},{8,0},{1,9},{9,1},{2,10},{10,2},{3,11},{11,3},{4,12},{12,4},... | collective-permute-start | bytes 786440 | tf_op jit(solution)/shard_map/ppermute | solution.py:61
  6.1 11.9 %collective-permute-start.11 = (bf16[128,1024]{1,0:T(8,128)(2,1)}, bf16[128,1024]{1,0:T(8,128)(2,1)S(1)}, u32[]{:S(2)}, u32[]{:S(2)}) collective-permute-start(bf16[128,1024]{1,0:T(8,128)(2,1)} %refs_0_.1), channel_id=1, source_target_pairs={{0,4},{2,6},{4,0},{6,2},{1,5},{3,7},{5,1},{7,3},{8,12},{10,14},{12... | collective-permute-start | bytes 786440 | tf_op jit(solution)/shard_map/ppermute | solution.py:61
  9.4 11.6 %collective-permute-start = (bf16[128,1024]{1,0:T(8,128)(2,1)}, bf16[128,1024]{1,0:T(8,128)(2,1)S(1)}, u32[]{:S(2)}, u32[]{:S(2)}) collective-permute-start(bf16[128,1024]{1,0:T(8,128)(2,1)} %refs_0_.1), channel_id=1, source_target_pairs={{0,1},{1,0},{2,3},{3,2},{4,5},{5,4},{6,7},{7,6},{8,9},{9,8},{10,11... | collective-permute-start | bytes 786440 | tf_op jit(solution)/shard_map/ppermute | solution.py:61
  10.9 10.0 %collective-permute-start.5 = (bf16[128,1024]{1,0:T(8,128)(2,1)}, bf16[128,1024]{1,0:T(8,128)(2,1)S(1)}, u32[]{:S(2)}, u32[]{:S(2)}) collective-permute-start(bf16[128,1024]{1,0:T(8,128)(2,1)} %refs_0_.1), channel_id=1, source_target_pairs={{0,6},{2,0},{4,2},{6,4},{1,7},{3,1},{5,3},{7,5},{8,14},{10,8},{12,... | collective-permute-start | bytes 786440 | tf_op jit(solution)/shard_map/ppermute | solution.py:61
  11.6 11.7 %collective-permute-start.4 = (bf16[128,1024]{1,0:T(8,128)(2,1)S(1)}, bf16[128,1024]{1,0:T(8,128)(2,1)S(1)}, u32[]{:S(2)}, u32[]{:S(2)}) collective-permute-start(bf16[128,1024]{1,0:T(8,128)(2,1)S(1)} %collective-permute-done.3.refs_0_), channel_id=1, source_target_pairs={{0,1},{1,0},{2,3},{3,2},{4,5},{5,4},{6,7},{7,6},{8,9},{9,8},{10,11... | collective-permute-start | bytes 786440 | tf_op jit(solution)/shard_map/ppermute | solution.py:61
  12.8 13.4 %collective-permute-start.9 = (bf16[128,1024]{1,0:T(8,128)(2,1)S(1)}, bf16[128,1024]{1,0:T(8,128)(2,1)S(1)}, u32[]{:S(2)}, u32[]{:S(2)}) collective-permute-start(bf16[128,1024]{1,0:T(8,128)(2,1)S(1)} %collective-permute-done.1.refs_2_), channel_id=1, source_target_pairs={{0,6},{2,0},{4,2},{6,4},{1,7},{3,1},{5,3},{7,5},{8,14},{10,8},{12,... | collective-permute-start | bytes 786440 | tf_op jit(solution)/shard_map/ppermute | solution.py:61
  18.0 9.6 %collective-permute-start.13 = (bf16[128,1024]{1,0:T(8,128)(2,1)S(1)}, bf16[128,1024]{1,0:T(8,128)(2,1)S(1)}, u32[]{:S(2)}, u32[]{:S(2)}) collective-permute-start(bf16[128,1024]{1,0:T(8,128)(2,1)S(1)} %collective-permute-done.11.refs_0_), channel_id=1, source_target_pairs={{0,8},{8,0},{1,9},{9,1},{2,10},{10,2},{3,11},{11,3},{4,12},{12,4},... | collective-permute-start | bytes 786440 | tf_op jit(solution)/shard_map/ppermute | solution.py:61
  20.9 9.9 %collective-permute-start.7 = (bf16[128,1024]{1,0:T(8,128)(2,1)S(1)}, bf16[128,1024]{1,0:T(8,128)(2,1)S(1)}, u32[]{:S(2)}, u32[]{:S(2)}) collective-permute-start(bf16[128,1024]{1,0:T(8,128)(2,1)S(1)} %collective-permute-done.1.refs_2_), channel_id=1, source_target_pairs={{0,2},{2,4},{4,6},{6,0},{1,3},{3,5},{5,7},{7,1},{8,10},{10,12},{12... | collective-permute-start | bytes 786440 | tf_op jit(solution)/shard_map/ppermute | solution.py:61
  20.9 10.0 %collective-permute-start.6 = (bf16[128,1024]{1,0:T(8,128)(2,1)S(1)}, bf16[128,1024]{1,0:T(8,128)(2,1)S(1)}, u32[]{:S(2)}, u32[]{:S(2)}) collective-permute-start(bf16[128,1024]{1,0:T(8,128)(2,1)S(1)} %collective-permute-done.5.refs_2_), channel_id=1, source_target_pairs={{0,1},{1,0},{2,3},{3,2},{4,5},{5,4},{6,7},{7,6},{8,9},{9,8},{10,11... | collective-permute-start | bytes 786440 | tf_op jit(solution)/shard_map/ppermute | solution.py:61
  23.4 9.9 %collective-permute-start.2 = (bf16[128,1024]{1,0:T(8,128)(2,1)S(1)}, bf16[128,1024]{1,0:T(8,128)(2,1)S(1)}, u32[]{:S(2)}, u32[]{:S(2)}) collective-permute-start(bf16[128,1024]{1,0:T(8,128)(2,1)S(1)} %collective-permute-done.1.refs_2_), channel_id=1, source_target_pairs={{0,1},{1,0},{2,3},{3,2},{4,5},{5,4},{6,7},{7,6},{8,9},{9,8},{10,11... | collective-permute-start | bytes 786440 | tf_op jit(solution)/shard_map/ppermute | solution.py:61
  26.1 9.0 %collective-permute-start.12 = (bf16[128,1024]{1,0:T(8,128)(2,1)S(1)}, bf16[128,1024]{1,0:T(8,128)(2,1)S(1)}, u32[]{:S(2)}, u32[]{:S(2)}) collective-permute-start(bf16[128,1024]{1,0:T(8,128)(2,1)S(1)} %collective-permute-done.11.refs_0_), channel_id=1, source_target_pairs={{0,1},{1,0},{2,3},{3,2},{4,5},{5,4},{6,7},{7,6},{8,9},{9,8},{10,11... | collective-permute-start | bytes 786440 | tf_op jit(solution)/shard_map/ppermute | solution.py:61
  53.9 21.4 %collective-permute-start.19 = (bf16[512,512]{1,0:T(8,128)(2,1)S(1)}, bf16[512,512]{1,0:T(8,128)(2,1)S(1)}, u32[]{:S(2)}, u32[]{:S(2)}) collective-permute-start(bf16[512,512]{1,0:T(8,128)(2,1)S(1)} %get-tuple-element.66), channel_id=1, source_target_pairs={{0,64},{64,0},{1,65},{65,1},{2,66},{66,2},{3,67},{67,3},{4,68},{68... | collective-permute-start | bytes 1572872 | tf_op jit(solution)/shard_map/ppermute | solution.py:61
  57.8 8.9 %collective-permute-start.15 = (bf16[2,136,512]{2,1,0:T(8,128)(2,1)S(1)}, bf16[2,136,512]{2,1,0:T(8,128)(2,1)S(1)}, u32[]{:S(2)}, u32[]{:S(2)}) collective-permute-start(bf16[2,136,512]{2,1,0:T(8,128)(2,1)S(1)} %get-tuple-element.60), channel_id=1, source_target_pairs={{0,32},{16,48},{32,0},{48,16},{1,33},{17,49},{33,1},{49,17},{2,34}... | collective-permute-start | bytes 835592 | tf_op jit(solution)/shard_map/ppermute | solution.py:61
  60.6 13.3 %collective-permute-start.16 = (bf16[2,136,512]{2,1,0:T(8,128)(2,1)S(1)}, bf16[2,136,512]{2,1,0:T(8,128)(2,1)S(1)}, u32[]{:S(2)}, u32[]{:S(2)}) collective-permute-start(bf16[2,136,512]{2,1,0:T(8,128)(2,1)S(1)} %get-tuple-element.61), channel_id=1, source_target_pairs={{0,16},{16,32},{32,48},{48,0},{1,17},{17,33},{33,49},{49,1},{2,18}... | collective-permute-start | bytes 835592 | tf_op jit(solution)/shard_map/ppermute | solution.py:61
  60.9 13.0 %collective-permute-start.17 = (bf16[2,136,512]{2,1,0:T(8,128)(2,1)S(1)}, bf16[2,136,512]{2,1,0:T(8,128)(2,1)S(1)}, u32[]{:S(2)}, u32[]{:S(2)}) collective-permute-start(bf16[2,136,512]{2,1,0:T(8,128)(2,1)S(1)} %get-tuple-element.62), channel_id=1, source_target_pairs={{0,48},{16,0},{32,16},{48,32},{1,49},{17,1},{33,17},{49,33},{2,50}... | collective-permute-start | bytes 835592 | tf_op jit(solution)/shard_map/ppermute | solution.py:61
  109.8 16.2 %all-to-all-start.2 = ((bf16[64,32,128]{2,1,0:T(8,128)(2,1)}), bf16[64,32,128]{2,1,0:T(8,128)(2,1)S(1)}, u32[]{:S(2)}, u32[]{:S(2)}) async-start(bf16[64,32,128]{2,1,0:T(8,128)(2,1)} %shard_map.65), calls=%async_computation.2 | async-start | bytes 1048576 | tf_op jit(solution)/shard_map/all_to_all | solution.py:378
  115.3 17.2 %collective-permute-start.25 = (bf16[128,1024]{1,0:T(8,128)(2,1)S(1)}, bf16[128,1024]{1,0:T(8,128)(2,1)S(1)}, u32[]{:S(2)}, u32[]{:S(2)}) collective-permute-start(bf16[128,1024]{1,0:T(8,128)(2,1)S(1)} %get-tuple-element.73.refs_0_), channel_id=1, source_target_pairs={{0,32},{16,48},{32,0},{48,16},{1,33},{17,49},{33,1},{49,17},{2,34}... | collective-permute-start | bytes 786440 | tf_op jit(solution)/shard_map/ppermute | solution.py:61
  118.2 14.4 %collective-permute-start.23 = (bf16[128,1024]{1,0:T(8,128)(2,1)S(1)}, bf16[128,1024]{1,0:T(8,128)(2,1)S(1)}, u32[]{:S(2)}, u32[]{:S(2)}) collective-permute-start(bf16[128,1024]{1,0:T(8,128)(2,1)S(1)} %get-tuple-element.73.refs_0_), channel_id=1, source_target_pairs={{0,64},{64,0},{1,65},{65,1},{2,66},{66,2},{3,67},{67,3},{4,68},{68... | collective-permute-start | bytes 786440 | tf_op jit(solution)/shard_map/ppermute | solution.py:61
  119.6 15.4 %collective-permute-start.29 = (bf16[128,1024]{1,0:T(8,128)(2,1)S(1)}, bf16[128,1024]{1,0:T(8,128)(2,1)S(1)}, u32[]{:S(2)}, u32[]{:S(2)}) collective-permute-start(bf16[128,1024]{1,0:T(8,128)(2,1)S(1)} %get-tuple-element.73.refs_0_), channel_id=1, source_target_pairs={{0,16},{16,32},{32,48},{48,0},{1,17},{17,33},{33,49},{49,1},{2,18}... | collective-permute-start | bytes 786440 | tf_op jit(solution)/shard_map/ppermute | solution.py:61
  126.0 21.4 %collective-permute-start.31 = (bf16[64,32,128]{2,1,0:T(8,128)(2,1)S(1)}, bf16[64,32,128]{2,1,0:T(8,128)(2,1)S(1)}, u32[]{:S(2)}, u32[]{:S(2)}) collective-permute-start(bf16[64,32,128]{2,1,0:T(8,128)(2,1)S(1)} %all-to-all-done.2.mine), channel_id=1, source_target_pairs={{0,1},{1,0},{2,3},{3,2},{4,5},{5,4},{6,7},{7,6},{8,9},{9,8},{10,11... | collective-permute-start | bytes 1572872 | tf_op jit(solution)/shard_map/ppermute | solution.py:61
  132.6 9.2 %collective-permute-start.26 = (bf16[128,1024]{1,0:T(8,128)(2,1)S(1)}, bf16[128,1024]{1,0:T(8,128)(2,1)S(1)}, u32[]{:S(2)}, u32[]{:S(2)}) collective-permute-start(bf16[128,1024]{1,0:T(8,128)(2,1)S(1)} %collective-permute-done.25.refs_2_), channel_id=1, source_target_pairs={{0,64},{64,0},{1,65},{65,1},{2,66},{66,2},{3,67},{67,3},{4,68},{68... | collective-permute-start | bytes 786440 | tf_op jit(solution)/shard_map/ppermute | solution.py:61
  132.6 9.2 %collective-permute-start.27 = (bf16[128,1024]{1,0:T(8,128)(2,1)S(1)}, bf16[128,1024]{1,0:T(8,128)(2,1)S(1)}, u32[]{:S(2)}, u32[]{:S(2)}) collective-permute-start(bf16[128,1024]{1,0:T(8,128)(2,1)S(1)} %collective-permute-done.23.refs_0_), channel_id=1, source_target_pairs={{0,16},{16,32},{32,48},{48,0},{1,17},{17,33},{33,49},{49,1},{2,18}... | collective-permute-start | bytes 786440 | tf_op jit(solution)/shard_map/ppermute | solution.py:61
  135.0 11.1 %collective-permute-start.24 = (bf16[128,1024]{1,0:T(8,128)(2,1)S(1)}, bf16[128,1024]{1,0:T(8,128)(2,1)S(1)}, u32[]{:S(2)}, u32[]{:S(2)}) collective-permute-start(bf16[128,1024]{1,0:T(8,128)(2,1)S(1)} %collective-permute-done.23.refs_0_), channel_id=1, source_target_pairs={{0,48},{16,0},{32,16},{48,32},{1,49},{17,1},{33,17},{49,33},{2,50}... | collective-permute-start | bytes 786440 | tf_op jit(solution)/shard_map/ppermute | solution.py:61
  (10 other events, 60.2 us)
